TPU v7x, 256 devices: a whole 4x4x8 slice. The times are simulated.
256 devices in a mesh: expert: 32 (over x, y, core), group: 8 (over z).
Axes of the slice: x: 4, y: 4, z: 8, core: 2. Of those that a mesh axis runs over, the one named last changes fastest.
Arguments:
- tokens: bfloat16 [2048, 7168], P(('expert', 'group')), may hold values from -6 to 6
- routes: int32 [2048, 8], P(('expert', 'group')), may hold values from 0 to 31, all different within a row; in each aligned block of 8 rows (0 to 7, 8 to 15, ...) at most 4 rows name the same one
- gate_weight: bfloat16 [32, 7168, 2048], P('expert', None, 'group'), may hold values from -0.0625 to 0.0625
- up_weight: bfloat16 [32, 7168, 2048], P('expert', None, 'group'), may hold values from -0.0625 to 0.0625
- down_weight: bfloat16 [32, 2048, 7168], P('expert', 'group'), may hold values from -6 to 6
- merge_group: int32 [32], replicated, may hold values from 0 to 7, as said below
- neuron_perm: int32 [32, 2048], P('expert', 'group'), may hold values from 0 to 2047, as said below
Outputs:
- merged_down: bfloat16 [8, 2048, 7168], P(None, 'group', 'expert')
Inputs may be any that keep to these rules, and one draw needn't show every extreme that they name: `routes`: among the rows of one device (8 rows), no expert is named by more than 4 rows. `merge_group`: every one of the 8 merge groups has at least one expert. `neuron_perm`: each row is a permutation of 0 to 2047 that keeps every hidden unit within its aligned block of 128.
All inputs are finite; a program needn't handle non-finite values.
Results may differ from a plain program's by a relative error of at most 0.0047.
Values may be sent and summed in bfloat16 or wider, within the bound.
A program may use at most 128 MiB of HBM per device.

v0:
```python
from functools import partial

import jax
import jax.numpy as jnp
from jax import lax
from jax.sharding import PartitionSpec as P

TOP = 8
NB = 128


off_weight = 0.75
ridge_eps = 1e-05


def make_slots(block_routes, block_tokens, experts, capacity):
    row_count = block_tokens.shape[0]
    flat_routes = block_routes.reshape(-1)
    onehot = (flat_routes[:, None] == jnp.arange(experts, dtype=jnp.int32)[None, :]).astype(
        jnp.int32
    )
    position = jnp.sum((jnp.cumsum(onehot, axis=0) - 1) * onehot, axis=1)
    target = flat_routes * capacity + position
    matches = target[None, :] == jnp.arange(experts * capacity, dtype=jnp.int32)[:, None]
    chooser = jnp.sum(
        matches.reshape(experts * capacity, row_count, -1).astype(jnp.float32), axis=2
    ).astype(jnp.bfloat16)
    return jnp.dot(chooser, block_tokens, preferred_element_type=jnp.float32).astype(jnp.bfloat16)


def activate(shard_piece, gate_weight, up_weight):
    gate_part = jnp.einsum(
        "ksjcd,jdf->ksjcf", shard_piece, gate_weight, preferred_element_type=jnp.float32
    )
    up_part = jnp.einsum(
        "ksjcd,jdf->ksjcf", shard_piece, up_weight, preferred_element_type=jnp.float32
    )
    return (jax.nn.silu(gate_part) * up_part).astype(jnp.bfloat16)


def build_system(summed):
    unit_matrix = jnp.eye(summed.shape[-1], dtype=jnp.float32)
    return (
        off_weight * summed + (1.0 - off_weight) * (summed * unit_matrix) + ridge_eps * unit_matrix
    )


def make_inverse(factor):
    unit_matrix = jnp.broadcast_to(jnp.eye(factor.shape[-1], dtype=jnp.float32), factor.shape)
    lower_inverse = lax.linalg.triangular_solve(factor, unit_matrix, left_side=True, lower=True)
    return jnp.einsum(
        "mbki,mbkj->mbij", lower_inverse, lower_inverse, precision=lax.Precision.HIGHEST
    )


def apply_inverse(inverse, right_side):
    return jnp.einsum("mbik,mbkd->mbid", inverse, right_side, precision=lax.Precision.HIGHEST)


def per_device(tokens, routes, gate_weight, up_weight, down_weight, merge_group, neuron_perm):
    expert_count = lax.axis_size("expert")
    group_count = lax.axis_size("group")
    local_experts = gate_weight.shape[0]
    experts = expert_count * local_experts
    row_count = tokens.shape[0]
    width = tokens.shape[1]
    unit_count = gate_weight.shape[2]
    capacity = max(2, row_count * TOP * 2 // (experts * local_experts))
    block_count = unit_count // NB
    column_count = width // expert_count
    groups = experts // 4
    slot_maker = partial(make_slots, experts=experts, capacity=capacity)
    own_slots = slot_maker(routes, tokens).reshape(expert_count, local_experts * capacity, width)
    arrived = lax.all_to_all(own_slots, "expert", split_axis=0, concat_axis=0, tiled=True)
    hidden = activate(
        lax.all_gather(
            arrived.reshape(1, expert_count, local_experts, capacity, width),
            "group",
            axis=0,
            tiled=True,
        ),
        gate_weight,
        up_weight,
    )
    hidden = hidden.reshape(group_count, expert_count, local_experts, capacity, block_count, NB)
    within = (
        neuron_perm.reshape(local_experts, block_count, NB) - lax.axis_index("group") * unit_count
    )
    within = within - (jnp.arange(block_count, dtype=jnp.int32) * NB)[None, :, None]
    selector = (
        within[:, :, None, :] == jnp.arange(NB, dtype=jnp.int32)[None, None, :, None]
    ).astype(jnp.bfloat16)
    aligned = jnp.einsum(
        "gejcbi,jbin->gejcbn", hidden, selector, preferred_element_type=jnp.float32
    ).astype(jnp.bfloat16)
    gram = jnp.einsum("gejcbi,gejcbk->jbik", aligned, aligned, preferred_element_type=jnp.float32)
    moved_rows = jnp.einsum(
        "jbin,jbid->jbnd",
        selector,
        down_weight.reshape(local_experts, block_count, NB, width),
        preferred_element_type=jnp.float32,
    )
    term_part = jnp.einsum("jbni,jbid->jbnd", gram, moved_rows, precision=lax.Precision.HIGHEST)
    owner_index = lax.axis_index("expert")
    own_groups = lax.dynamic_slice_in_dim(merge_group, owner_index * local_experts, local_experts)
    own_onehot = (own_groups[:, None] == jnp.arange(groups, dtype=jnp.int32)[None, :]).astype(
        jnp.float32
    )
    placed = jnp.einsum("jm,jbik->mbik", own_onehot, gram, precision=lax.Precision.HIGHEST)
    group_gram = lax.psum(placed, "expert")
    inverse = make_inverse(jnp.linalg.cholesky(build_system(group_gram)))
    shaped_terms = term_part.reshape(local_experts, block_count, NB, expert_count, column_count)
    collected = lax.all_to_all(shaped_terms, "expert", split_axis=3, concat_axis=0, tiled=True)
    all_onehot = (merge_group[:, None] == jnp.arange(groups, dtype=jnp.int32)[None, :]).astype(
        jnp.float32
    )
    summed = jnp.einsum(
        "em,ebnd->mbnd", all_onehot, collected[:, :, :, 0, :], precision=lax.Precision.HIGHEST
    )
    merged = apply_inverse(inverse, summed)
    return merged.reshape(groups, unit_count, column_count).astype(jnp.bfloat16)


def solution(mesh):
    in_specs = (
        P(("expert", "group"), None),
        P(("expert", "group"), None),
        P("expert", None, "group"),
        P("expert", None, "group"),
        P("expert", "group", None),
        P(),
        P("expert", "group"),
    )
    out_specs = P(None, "group", "expert")
    return jax.shard_map(
        per_device, mesh=mesh, in_specs=in_specs, out_specs=out_specs, check_vma=False
    )
```

profile of v0, /device:TPU:1, one launch (start us, length us, event | category | flops | bytes accessed | tf_op | source)
XLA Modules:
  0.0 783.2 jit_solution(4557623676575485270)
XLA Ops:
  6.5 0.8 eq.91
  7.8 0.7 multiply_add_fusion
  8.6 0.7 convolution_convert_fusion
  9.3 1.7 reshape.138
  10.9 34.1 %all_to_all.20 = bf16[32,4,7168]{2,1,0:T(4,128)(2,1)S(1)} all-to-all(bf16[32,4,7168]{2,1,0:T(4,128)(2,1)} %reshape.138), channel_id=1, replica_groups=mesh['expert'=32,'group'=8] {'expert'}, dimensions={0} | all-to-all | bytes 3670016 | tf_op jit(solution)/shard_map/all_to_all | solution.py:74
  45.0 1.8 copy.66
  46.9 6.1 fusion.44
  53.1 145.8 %all-gather.3.cloned.1.call-done = bf16[256,4,7168]{2,0,1:T(8,128)(2,1)} async-done(((bf16[32,4,7168]{2,0,1:T(8,128)(2,1)}), bf16[256,4,7168]{2,0,1:T(8,128)(2,1)}) %all-gather.3.cloned.1.call-update) | async-done | bytes 14680080 | tf_op jit(solution)/shard_map/all_gather | solution.py:76
  198.9 8.5 %fusion.14 = f32[8,32,1,4,256]{4,1,3,0,2:T(8,128)S(1)} fusion(bf16[1,7168,256]{2,1,0:T(8,128)(2,1)} %param.9, bf16[8,32,4,7168]{3,1,0,2:T(8,128)(2,1)} %bitcast.99), kind=kOutput, calls=%fused_computation.13 | convolution fusion | flops 3758096384 | bytes 19398656 | tf_op jit(solution)/shard_map/ksjcd,jdf->ksjcf/dot_general | solution.py:32
  207.4 1.9 copy-done.5
  209.3 6.0 fusion.32
  215.5 0.4 fusion.37
  215.8 0.3 convolution_bitcast_fusion
  216.2 14.0 %fusion.57 = f32[2,128,7168]{1,2,0:T(8,128)S(1)} fusion(f32[2,128,128]{2,1,0:T(8,128)S(1)} %convolution_bitcast_fusion, f32[2,128,7168]{2,1,0:T(8,128)} %fusion.44), kind=kOutput, calls=%fused_computation.58 | convolution fusion | flops 2818572288 | bytes 14811136 | tf_op jit(solution)/shard_map/jbni,jbid->jbnd/dot_general | solution.py:103
  230.2 3.7 copy.83
  233.9 7.9 %all-to-all-start.1 = ((f32[1,2,128,32,224]{2,4,1,0,3:T(8,128)}), f32[1,2,128,32,224]{2,4,1,0,3:T(8,128)}, u32[]{:S(2)}, u32[]{:S(2)}) async-start(f32[1,2,128,32,224]{2,4,1,0,3:T(8,128)} %copy.83), calls=%async_computation.1 | async-start | bytes 14680064 | tf_op jit(solution)/shard_map/all_to_all | solution.py:113
  241.8 0.6 dynamic_slice.3
  242.4 0.6 compare_convert_fusion
  243.2 1.2 broadcast_multiply_fusion
  244.6 167.6 %all-reduce.2.cloned.1.call-done = f32[8,2,128,128]{2,3,1,0:T(8,128)} async-done(((f32[8,2,128,128]{2,3,1,0:T(8,128)}), f32[8,2,128,128]{2,3,1,0:T(8,128)}) %all-reduce.2.cloned.1.call-update) | async-done | bytes 1048592 | tf_op jit(solution)/shard_map/psum | solution.py:110
  412.2 1.5 add_add_fusion
  413.7 0.3 copy.76
  414.1 0.2 fusion.40
  414.3 187.8 %custom-call.7 = f32[8,2,128,128]{3,2,1,0:T(8,128)S(1)} custom-call(f32[8,2,128,128]{3,2,1,0:T(8,128)S(1)} %fusion.40), custom_call_target="Cholesky" | custom-call | tf_op jit(solution)/shard_map/jit(cholesky)/cholesky | solution.py:111
  602.2 0.2 compare_reduce_fusion
  602.4 0.2 select_bitcast_fusion
  602.6 157.2 %custom-call.8 = f32[8,2,1,128,128]{3,4,2,1,0:T(8,128)S(1)} custom-call(f32[8,2,1,128,128]{4,3,2,1,0:T(8,128)S(1)} %select_bitcast_fusion), custom_call_target="InvertDiagBlocksLowerTriangular" | custom-call | tf_op jit(solution)/shard_map/triangular_solve | solution.py:50
  759.8 1.8 fusion.38
  761.7 1.8 fusion.56
  763.5 9.7 %fusion.4 = f32[8,2,128,224]{2,0,3,1:T(8,128)S(1)} fusion(f32[1,2,128,32,224]{2,4,1,0,3:T(8,128)} %all-to-all-done.1, s32[32]{0:T(128)S(1)} %copy-done.4), kind=kOutput, calls=%fused_computation.5 | convolution fusion | flops 176161024 | bytes 9175168 | tf_op jit(solution)/shard_map/em,ebnd->mbnd/dot_general | solution.py:117
  773.3 2.0 fusion.29
  775.3 1.1 copy.127
  (33 shorter events, 1.2 us)
Async XLA Ops:
  6.5 2.0 copy-start
  6.5 192.3 %all-gather.3.cloned.1.call-start = ((), (), s32[]{:S(2)}) async-start(), calls=%async_computation.3 | async-start | bytes 16515072 | tf_op jit(solution)/shard_map/all_gather | solution.py:76
  45.0 1.9 copy-start.3
  198.9 10.4 %copy-start.5 = (bf16[256,4,7168]{2,0,1:T(8,128)(2,1)S(1)}, bf16[256,4,7168]{2,0,1:T(8,128)(2,1)}, u32[]{:S(2)}) copy-start(bf16[256,4,7168]{2,0,1:T(8,128)(2,1)} %all-gather.3.cloned.1.call-done) | copy-start | bytes 44040196
  233.9 7.9 %copy-start.4 = (s32[32]{0:T(128)S(1)}, s32[32]{0:T(128)}, u32[]{:S(2)}) copy-start(s32[32]{0:T(128)} %param.12) | copy-start | bytes 388
  233.9 529.7 %all-to-all-start.1 = ((f32[1,2,128,32,224]{2,4,1,0,3:T(8,128)}), f32[1,2,128,32,224]{2,4,1,0,3:T(8,128)}, u32[]{:S(2)}, u32[]{:S(2)}) async-start(f32[1,2,128,32,224]{2,4,1,0,3:T(8,128)} %copy.83), calls=%async_computation.1 | async-start | bytes 14680064 | tf_op jit(solution)/shard_map/all_to_all | solution.py:113
  241.8 170.5 %all-reduce.2.cloned.1.call-start = ((), (), s32[]{:S(2)}) async-start(), calls=%async_computation.2 | async-start | bytes 2097152 | tf_op jit(solution)/shard_map/psum | solution.py:110
  412.2 1.8 copy-start.2
  763.5 12.9 %copy-start.1 = (bf16[8,7168]{1,0:T(8,128)(2,1)S(1)}, bf16[8,7168]{1,0:T(8,128)(2,1)}, u32[]{:S(2)}) copy-start(bf16[8,7168]{1,0:T(8,128)(2,1)} %param.7) | copy-start | bytes 344068
Sparse Core Ops, SparseCore 0:
  46.9 151.8 all-gather.2
  245.8 166.4 all-reduce.1
where the time goes:
time: 784 us; the launch traced here: 783 us
  other arithmetic  350 us (45%)
  waiting for transfers between devices  313 us (40%)
  matrix products  51.5 us (7%)
  blocking collectives  34.1 us (4%)
  between operations  13.7 us (2%)
  local copies, waits for them, and re-layouts  12.4 us (2%)
  starting transfers between devices  7.92 us (1%)
    another operation x4, other arithmetic, per_device(): inverse = make_inverse(jnp.linalg.cholesky(build_system(group_gram)))  188 us
    psum x1, waiting for transfers between devices, per_device(): group_gram = lax.psum(placed, 'expert')  168 us
    another operation x3, other arithmetic, make_inverse(): lax.linalg.triangular_solve(factor, unit_matrix, left_side=True, lower=True)  157 us
    all_gather x1, waiting for transfers between devices, per_device(): lax.all_gather(arrived.reshape(1, expert_count, local_experts, capacity,...  146 us
    all_to_all x1, blocking collectives, per_device(): lax.all_to_all(own_slots, 'expert', split_axis=0, concat_axis=0, tiled=True)  34.1 us
  transfers between devices with their start and end apart: 3, of which 2 were waited for; matrix products, arithmetic and copies ran while one was open for 46% of the time, Pallas kernels for 0%

commit v1 on v0

v1 whole, which is shorter than its diff:
```python
from functools import partial

import jax
import jax.numpy as jnp
from jax import lax
from jax.experimental import pallas as pl
from jax.experimental.pallas import tpu as pltpu
from jax.sharding import PartitionSpec as P

NB = 128
F32 = jnp.float32
BF16 = jnp.bfloat16
MESH = pl.DeviceIdType.MESH
XN, YN, ZN = 4, 4, 8


def place(x, y, core):
    return (x * YN + y) * 2 + core


def gather_kernel(part, width, tok_ref, gate_ref, up_ref, out_ref, bufx, bufy, bufz, weights, acc, lhs,
                  send_sem, recv_sem, own_sem, wsem, wsend, wrecv):
    expert = lax.axis_index("expert")
    z = lax.axis_index("group")
    core = lax.rem(expert, 2)
    y = lax.rem(lax.div(expert, 2), YN)
    x = lax.div(expert, 2 * YN)
    units = gate_ref.shape[1]

    def device(axis, shift):
        px, py, pz, pc = x, y, z, core
        if axis == "x":
            px = lax.rem(x + XN + shift, XN)
        elif axis == "y":
            py = lax.rem(y + YN + shift, YN)
        elif axis == "z":
            pz = lax.rem(z + ZN + shift, ZN)
        else:
            pc = 1 - core
        return (place(px, py, pc), pz)

    colors = (
        (bufx, (("z", ZN, z), ("y", YN, y), ("x", XN, x)), (x, y)),
        (bufy, (("z", ZN, z), ("x", XN, x), ("y", YN, y)), (y, x)),
        (bufz, (("y", YN, y), ("x", XN, x), ("z", ZN, z)), (z, x)),
    )
    columns = (0, part, 2 * part)
    half_cols = (part // 256) * 128 + 128

    barrier = pltpu.get_barrier_semaphore()
    neighbours = [device(a, s) for a in "xyz" for s in (1, -1)] + [device("core", 0)]
    for other in neighbours:
        pl.semaphore_signal(barrier, inc=1, device_id=other, device_id_type=MESH)
    pl.semaphore_wait(barrier, len(neighbours))

    def unit(color, stage, pos, half=None):
        buf, _, (first, second) = colors[color]
        if stage == 0:
            if half is None:
                return buf.at[first, second, pos]
            cols = pl.ds(0, half_cols) if half == 0 else pl.ds(half_cols, part - half_cols)
            return buf.at[first, second, pos, :, cols]
        lead = (first, pos) if stage == 1 else (pos,)
        size = buf.shape[len(lead)]
        if half is not None:
            lead = lead + (pl.ds(half * (size // 2), size // 2),)
        return buf.at[lead]

    started = {}

    def start(color, stage, step):
        axis, n, pos = colors[color][1][stage]
        for way, sign in ((0, 1), (1, -1)):
            half = way if step == n // 2 else None
            which = lax.rem(pos + n - sign * (step - 1), n)
            dst = unit(color, stage, which, half)
            src = dst
            if stage == 0 and step == 1:
                src = tok_ref.at[:, pl.ds(columns[color], part)]
            copy = pltpu.make_async_remote_copy(
                src_ref=src,
                dst_ref=dst,
                send_sem=send_sem.at[color, stage, way, step - 1],
                recv_sem=recv_sem.at[color, stage, way, step - 1],
                device_id=device(axis, sign),
                device_id_type=MESH,
            )
            copy.start()
            started[color, stage, way, step] = copy

    def arrive(color, stage, step):
        for way in (0, 1):
            started[color, stage, way, step].wait_recv()

    for color in range(3):
        start(color, 0, 1)
    own = []
    for color in range(3):
        axis, n, pos = colors[color][1][0]
        copy = pltpu.make_async_copy(tok_ref.at[:, pl.ds(columns[color], part)], unit(color, 0, pos), own_sem.at[color])
        copy.start()
        own.append(copy)
    moves = []
    for j, ref in enumerate((gate_ref, up_ref)):
        local = pltpu.make_async_copy(ref, weights.at[core * 2 + j], wsem.at[j])
        local.start()
        remote = pltpu.make_async_remote_copy(
            src_ref=ref,
            dst_ref=weights.at[core * 2 + j],
            send_sem=wsend.at[j],
            recv_sem=wrecv.at[j],
            device_id=device("core", 0),
            device_id_type=MESH,
        )
        remote.start()
        moves.append((local, remote))
    acc[...] = jnp.zeros_like(acc)
    for copy in own:
        copy.wait()
    for step in range(1, 5):
        for color in (0, 1):
            arrive(color, 0, step)
            if step < 4:
                start(color, 0, step + 1)
            else:
                start(color, 1, 1)
        stage, sub = (0, step) if step <= 2 else (1, step - 2)
        arrive(2, stage, sub)
        if sub == 1:
            start(2, stage, 2)
        elif stage == 0:
            start(2, 1, 1)
        else:
            start(2, 2, 1)

    def multiply(plane_rows, depth, first_row, slot):
        def per_column(n, carry):
            w = weights[n, pl.ds(first_row, depth), :]
            value = jnp.dot(lhs[0:plane_rows, 0:depth], w, preferred_element_type=F32)
            if slot[0] == "x":
                acc[n, slot[1]] += value.reshape(YN, ZN, 8, units)
            elif slot[0] == "y":
                acc[n, :, slot[1]] += value.reshape(XN, ZN, 8, units)
            else:
                acc[n, :, :, slot[1]] += value.reshape(XN, YN, 8, units)
            return carry

        lax.fori_loop(0, 4, per_column, 0)

    def take(color, plane):
        buf = colors[color][0]
        depth = part if color < 2 else width - 2 * part
        rows = 256 if color < 2 else 128
        value = buf[plane, :, :, :, 0:depth].astype(F32)
        lhs[0:rows, 0:depth] = value.reshape(rows, depth).astype(BF16)
        multiply(rows, depth, columns[color], ("xyz"[color], plane))

    def near(axis, shift):
        n, pos = {"x": (XN, x), "y": (YN, y), "z": (ZN, z)}[axis]
        return lax.rem(pos + n + shift, n)

    for local, remote in moves:
        local.wait()
        remote.wait_recv()
    take(2, z)
    for color in (0, 1):
        arrive(color, 1, 1)
        start(color, 1, 2)
    for color in (0, 1):
        arrive(color, 1, 2)
        start(color, 2, 1)
    take(0, x)
    take(1, y)
    arrive(2, 2, 1)
    start(2, 2, 2)
    take(2, near("z", 1))
    take(2, near("z", -1))
    arrive(2, 2, 2)
    start(2, 2, 3)
    take(2, near("z", 2))
    take(2, near("z", -2))
    for color in (0, 1):
        arrive(color, 2, 1)
        start(color, 2, 2)
    take(0, near("x", 1))
    arrive(2, 2, 3)
    start(2, 2, 4)
    take(0, near("x", -1))
    take(1, near("y", 1))
    take(1, near("y", -1))
    take(2, near("z", 3))
    take(2, near("z", -3))
    arrive(2, 2, 4)
    take(2, near("z", 4))
    arrive(0, 2, 2)
    take(0, near("x", 2))
    arrive(1, 2, 2)
    take(1, near("y", 2))

    blocks = units // NB
    out_ref[...] = jnp.zeros_like(out_ref)
    spare = width - 2 * part

    def finish(i, carry):
        px, p = lax.div(i, 2), lax.rem(i, 2)
        named = (place(x, y, 0) + p).astype(F32)
        gate = acc[2 * p, px].reshape(256, units)
        up = acc[2 * p + 1, px].reshape(256, units)
        listed = jnp.concatenate(
            [bufz[:, px, py, :, spare : spare + NB].astype(F32).reshape(ZN * 8, NB) for py in range(YN)], axis=0
        )
        chosen = jnp.max(jnp.where(listed == named, 1.0, 0.0), axis=1, keepdims=True)
        value = gate / (1.0 + jnp.exp(-gate)) * up
        hidden = jnp.where(chosen > 0.5, value, 0.0).astype(BF16)
        for b in range(blocks):
            piece = hidden[:, b * NB : (b + 1) * NB]
            out_ref[p, b] += lax.dot_general(piece, piece, (((0,), (0,)), ((), ())), preferred_element_type=F32)
        return carry

    lax.fori_loop(0, 2 * XN, finish, 0)
    for copy in started.values():
        copy.wait_send()
    for _, remote in moves:
        remote.wait_send()


def gather_grams(tokens, routes, gate_weight, up_weight):
    rows, width = tokens.shape
    units = gate_weight.shape[1]
    listed = jnp.pad(routes.astype(BF16), ((0, 0), (0, NB - routes.shape[1])), constant_values=-1)
    wide = jnp.concatenate([tokens, listed], axis=1)
    part = (width + NB) // 3
    return pl.pallas_call(
        partial(gather_kernel, part, width),
        out_shape=jax.ShapeDtypeStruct((2, units // NB, NB, NB), F32),
        in_specs=[pl.BlockSpec(memory_space=pl.ANY)] * 3,
        out_specs=pl.BlockSpec(memory_space=pltpu.VMEM),
        scratch_shapes=[
            pltpu.VMEM((XN, YN, ZN, 8, part), BF16),
            pltpu.VMEM((YN, XN, ZN, 8, part), BF16),
            pltpu.VMEM((ZN, XN, YN, 8, part), BF16),
            pltpu.VMEM((4, width, units), BF16),
            pltpu.VMEM((4, XN, YN, ZN, 8, units), F32),
            pltpu.VMEM((256, part), BF16),
            pltpu.SemaphoreType.DMA((3, 3, 2, 4)),
            pltpu.SemaphoreType.DMA((3, 3, 2, 4)),
            pltpu.SemaphoreType.DMA((3,)),
            pltpu.SemaphoreType.DMA((2,)),
            pltpu.SemaphoreType.DMA((2,)),
            pltpu.SemaphoreType.DMA((2,)),
        ],
        compiler_params=pltpu.CompilerParams(collective_id=0, has_side_effects=True, vmem_limit_bytes=60 * 1024 * 1024),
        name="gather_grams",
    )(wide, gate_weight, up_weight)


MGROUPS = 8
OFF_WEIGHT = 0.75
RIDGE = 1e-05
OCT = 8


def split_two(value):
    high = value.astype(BF16)
    return high, (value - high.astype(F32)).astype(BF16)


def dot3(left, right, contract=(1, 0)):
    lh, ll = split_two(left)
    rh, rl = split_two(right)
    dims = (((contract[0],), (contract[1],)), ((), ()))
    part = partial(lax.dot_general, dimension_numbers=dims, preferred_element_type=F32)
    return part(lh, rh) + part(lh, rl) + part(ll, rh)


def lane_pick(value, k):
    where = jnp.full(value.shape, k, jnp.int32)
    return jnp.take_along_axis(value, where, axis=1, mode="promise_in_bounds")


def factor(state, systems):
    lanes = lax.broadcasted_iota(jnp.int32, (systems, NB), 1)
    for octet in range(NB // OCT):

        def step(s, carry):
            k = octet * OCT + s
            row = state[k]
            inverse = 1.0 / lane_pick(row, k)
            scaled = (row + (lanes == k).astype(F32)) * inverse
            for t in range(1, OCT):
                i = octet * OCT + t
                other = state[i]
                keep = jnp.where(t > s, 1.0, 0.0)
                state[i] = other - lane_pick(other, k) * (scaled * keep)
            for i in range((octet + 1) * OCT, NB):
                other = state[i]
                state[i] = other - lane_pick(other, k) * scaled
            return carry

        lax.fori_loop(0, OCT, step, 0)


def solve_kernel(group_of, gram_ref, moved_ref, out_ref, sums, state, scales, moved_buf, terms, sem):
    blocks, experts = gram_ref.shape[0], gram_ref.shape[1]
    systems = MGROUPS * blocks
    fetch = pltpu.make_async_copy(moved_ref, moved_buf, sem)
    fetch.start()
    sums[...] = jnp.zeros_like(sums)
    terms[...] = jnp.zeros_like(terms)

    def add_gram(e, carry):
        group = group_of[e]
        for b in range(blocks):
            where = group * blocks + b
            sums[where] = sums[where] + gram_ref[b, e]
        return carry

    lax.fori_loop(0, experts, add_gram, 0)
    rows = lax.broadcasted_iota(jnp.int32, (NB, NB), 0)
    lanes = lax.broadcasted_iota(jnp.int32, (NB, NB), 1)
    same = rows == lanes
    for i in range(systems):
        summed = sums[i]
        diagonal = jnp.where(same, summed + RIDGE, 0.0)
        across = lax.rsqrt(jnp.sum(diagonal, axis=0, keepdims=True))
        down = lax.rsqrt(jnp.sum(diagonal, axis=1, keepdims=True))
        scales[i] = jnp.broadcast_to(across, (8, NB))
        state[:, i, :] = jnp.where(same, diagonal, OFF_WEIGHT * summed) * down * across
    factor(state, systems)
    fetch.wait()

    def add_term(e, carry):
        group = group_of[e]
        for b in range(blocks):
            where = group * blocks + b
            high, low = split_two(gram_ref[b, e])
            moved = moved_buf[e, b]
            terms[where] = terms[where] + (
                jnp.dot(moved, high, preferred_element_type=F32)
                + jnp.dot(moved, low, preferred_element_type=F32)
            )
        return carry

    lax.fori_loop(0, experts, add_term, 0)
    for m in range(MGROUPS):
        for b in range(blocks):
            i = m * blocks + b
            full = state[:, i, :]
            lower = jnp.where(lanes < rows, full, jnp.where(same, 1.0, 0.0))
            inverse = 1.0 / jnp.sum(jnp.where(same, full, 0.0), axis=0, keepdims=True)
            scale = scales[i, 0:1, :]
            half = dot3(terms[i] * scale, lower, (1, 1)) * inverse
            merged = dot3(half, lower, (1, 0)) * scale
            out_ref[m, :, b * NB : (b + 1) * NB] = merged.astype(BF16)


def solve(merge_group, grams, moved):
    blocks, experts = grams.shape[0], grams.shape[1]
    columns = moved.shape[2]
    systems = MGROUPS * blocks
    return pl.pallas_call(
        solve_kernel,
        out_shape=jax.ShapeDtypeStruct((MGROUPS, columns, blocks * NB), BF16),
        grid_spec=pltpu.PrefetchScalarGridSpec(
            num_scalar_prefetch=1,
            grid=(),
            in_specs=[
                pl.BlockSpec(memory_space=pltpu.VMEM),
                pl.BlockSpec(memory_space=pl.ANY),
            ],
            out_specs=pl.BlockSpec(memory_space=pltpu.VMEM),
            scratch_shapes=[
                pltpu.VMEM((systems, NB, NB), F32),
                pltpu.VMEM((NB, systems, NB), F32),
                pltpu.VMEM((systems, 8, NB), F32),
                pltpu.VMEM(moved.shape, BF16),
                pltpu.VMEM((systems, columns, NB), F32),
                pltpu.SemaphoreType.DMA,
            ],
        ),
        name="solve",
    )(merge_group, grams, moved)


def dot_exact(left, right, contract, split_left):
    value, one_hot = (left, right) if split_left else (right, left)
    first = value.astype(BF16)
    rest = value - first.astype(F32)
    second = rest.astype(BF16)
    third = (rest - second.astype(F32)).astype(BF16)
    dims = (((contract[0],), (contract[1],)), ((), ()))
    total = None
    for part in (first, second, third):
        pair = (part, one_hot) if split_left else (one_hot, part)
        term = lax.dot_general(*pair, dims, preferred_element_type=F32)
        total = term if total is None else total + term
    return total


def exchange_kernel(part_ref, selector_ref, gram_ref, inbox, send_sem, recv_sem, relay_send, relay_recv, pair_sem):
    expert = lax.axis_index("expert")
    z = lax.axis_index("group")
    core = lax.rem(expert, 2)
    y = lax.rem(lax.div(expert, 2), YN)
    x = lax.div(expert, 2 * YN)
    partner = (place(x, y, 1 - core), z)

    def device(axis, shift):
        if axis == "x":
            return (place(lax.rem(x + XN + shift, XN), y, core), z)
        return (place(x, lax.rem(y + YN + shift, YN), core), z)

    barrier = pltpu.get_barrier_semaphore()
    neighbours = [device(a, s) for a in "xy" for s in (1, -1)] + [partner]
    for other in neighbours:
        pl.semaphore_signal(barrier, inc=1, device_id=other, device_id_type=MESH)
    pl.semaphore_wait(barrier, len(neighbours))

    swap = pltpu.make_async_remote_copy(
        src_ref=part_ref.at[1 - core],
        dst_ref=inbox,
        send_sem=pair_sem.at[0],
        recv_sem=pair_sem.at[1],
        device_id=partner,
        device_id_type=MESH,
    )
    swap.start()
    blocks = part_ref.shape[1]
    axes = (("x", x), ("y", y))
    swap.wait_recv()
    for b in range(blocks):
        summed = part_ref[core, b] + inbox[b]
        turned = dot_exact(selector_ref[b], summed, (0, 0), False)
        gram_ref[b, x, y, core] = dot_exact(turned, selector_ref[b], (1, 0), True)

    def unit(b, stage, pos, half=None):
        along = axes[b] if stage == 0 else axes[1 - b]
        if stage == 0:
            lead = (b, pos, y, core) if along[0] == "x" else (b, x, pos, core)
            return gram_ref.at[lead + ((pl.ds(half * (NB // 2), NB // 2),) if half is not None else ())]
        other = pl.ds(0, XN) if half is None else pl.ds(half * (XN // 2), XN // 2)
        lead = (b, pos, other, core) if along[0] == "x" else (b, other, pos, core)
        return gram_ref.at[lead]

    started = {}

    def start(b, stage, step):
        axis, pos = axes[b] if stage == 0 else axes[1 - b]
        for way, sign in ((0, 1), (1, -1)):
            half = way if step == 2 else None
            ref = unit(b, stage, lax.rem(pos + XN - sign * (step - 1), XN), half)
            copy = pltpu.make_async_remote_copy(
                src_ref=ref,
                dst_ref=ref,
                send_sem=send_sem.at[b, stage, way, step - 1],
                recv_sem=recv_sem.at[b, stage, way, step - 1],
                device_id=device(axis, sign),
                device_id_type=MESH,
            )
            copy.start()
            started[b, stage, way, step] = copy

    def arrive(b, stage, step):
        for way in (0, 1):
            started[b, stage, way, step].wait_recv()

    relays = []

    def relay(b, shift):
        axis, pos = axes[1 - b]
        ref = unit(b, 1, lax.rem(pos + shift, XN))
        copy = pltpu.make_async_remote_copy(
            src_ref=ref,
            dst_ref=ref,
            send_sem=relay_send.at[b, shift],
            recv_sem=relay_recv.at[b, shift],
            device_id=partner,
            device_id_type=MESH,
        )
        copy.start()
        relays.append(copy)

    for b in range(blocks):
        start(b, 0, 1)
    for b in range(blocks):
        arrive(b, 0, 1)
        start(b, 0, 2)
    for b in range(blocks):
        arrive(b, 0, 2)
        start(b, 1, 1)
    for b in range(blocks):
        relay(b, 0)
    for b in range(blocks):
        arrive(b, 1, 1)
        start(b, 1, 2)
    for b in range(blocks):
        relay(b, 1)
        relay(b, 3)
    for b in range(blocks):
        arrive(b, 1, 2)
        relay(b, 2)
    for copy in relays:
        copy.wait_recv()
        copy.wait_send()
    for copy in started.values():
        copy.wait_send()
    swap.wait_send()


def exchange(partials, selector):
    blocks = partials.shape[1]
    return pl.pallas_call(
        exchange_kernel,
        out_shape=jax.ShapeDtypeStruct((blocks, XN, YN, 2, NB, NB), F32),
        in_specs=[pl.BlockSpec(memory_space=pltpu.VMEM)] * 2,
        out_specs=pl.BlockSpec(memory_space=pltpu.VMEM),
        scratch_shapes=[
            pltpu.VMEM((blocks, NB, NB), F32),
            pltpu.SemaphoreType.DMA((blocks, 2, 2, 2)),
            pltpu.SemaphoreType.DMA((blocks, 2, 2, 2)),
            pltpu.SemaphoreType.DMA((blocks, 4)),
            pltpu.SemaphoreType.DMA((blocks, 4)),
            pltpu.SemaphoreType.DMA((2,)),
        ],
        compiler_params=pltpu.CompilerParams(collective_id=1, has_side_effects=True),
        name="exchange_grams",
    )(partials, selector)


def per_device(tokens, routes, gate_weight, up_weight, down_weight, merge_group, neuron_perm):
    experts = lax.axis_size("expert")
    units = gate_weight.shape[2]
    blocks = units // NB
    width = tokens.shape[1]
    columns = width // experts
    start = lax.axis_index("group") * units + jnp.arange(blocks, dtype=jnp.int32) * NB
    within = neuron_perm.reshape(blocks, NB) - start[:, None]
    selector = (within[:, None, :] == jnp.arange(NB, dtype=jnp.int32)[None, :, None]).astype(BF16)
    moved = jnp.einsum(
        "bid,bin->bdn", down_weight.reshape(blocks, NB, width), selector, preferred_element_type=F32
    ).astype(BF16)
    partials = gather_grams(tokens, routes, gate_weight[0], up_weight[0])
    shaped = moved.reshape(1, blocks, experts, columns, NB)
    spread = lax.all_to_all(shaped, "expert", split_axis=2, concat_axis=0, tiled=True)
    spread = spread.reshape(experts, blocks, columns, NB)
    grams = exchange(partials, selector).reshape(blocks, experts, NB, NB)
    return jnp.swapaxes(solve(merge_group, grams, spread), 1, 2)


def solution(mesh):
    in_specs = (
        P(("expert", "group"), None),
        P(("expert", "group"), None),
        P("expert", None, "group"),
        P("expert", None, "group"),
        P("expert", "group", None),
        P(),
        P("expert", "group"),
    )
    return jax.shard_map(
        per_device, mesh=mesh, in_specs=in_specs, out_specs=P(None, "group", "expert"), check_vma=False
    )
```

time: 784 us -> 222 us (0.28)
  other arithmetic: 350 us -> 2.06 us
  waiting for transfers between devices: 313 us -> 0.01 us
  Pallas kernels: 0 us -> 196 us
  matrix products: 51.5 us -> 5.03 us
  blocking collectives: 34.1 us -> 0 us
  between operations: 13.7 us -> 0.22 us
    another operation x9 -> x0, other arithmetic: 346 us -> none  [the longest x4 188 us: per_device(): inverse = make_inverse(jnp.linalg.cholesky(build_system(group_gram)))]
    pallas_call x0 -> x3, Pallas kernels: none -> 196 us  [the longest x1 115 us: gather_grams(): pl.pallas_call(partial(gather_kernel, part, width), out_shape=jax.ShapeDt...]
    psum x1 -> x0, waiting for transfers between devices: 168 us -> none  [per_device(): group_gram = lax.psum(placed, 'expert')]
    all_gather x1 -> x0, waiting for transfers between devices: 146 us -> none  [per_device(): lax.all_gather(arrived.reshape(1, expert_count, local_experts, capacity,...]
    dot_general x10 -> x1, matrix products: 49.7 us -> 5.03 us  [per_device(): jnp.einsum('bid,bin->bdn', down_weight.reshape(blocks, NB, width), select...]
    all_to_all x1 -> x0, blocking collectives: 34.1 us -> none  [per_device(): lax.all_to_all(own_slots, 'expert', split_axis=0, concat_axis=0, tiled=True)]
  transfers between devices with their start and end apart: 3 -> 1, of which waited for: 2 -> 0; matrix products, arithmetic and copies ran while one was open for 46% -> 1% of each run, Pallas kernels for 0% -> 68%
where the time goes in v1:
time: 222 us
  Pallas kernels  196 us (88%)
  local copies, waits for them, and re-layouts  10.3 us (5%)
  starting transfers between devices  8.76 us (4%)
  matrix products  5.03 us (2%)
    pallas_call x1, Pallas kernels, gather_grams(): pl.pallas_call(partial(gather_kernel, part, width), out_shape=jax.ShapeDt...  115 us
    pallas_call x1, Pallas kernels, solve(): pl.pallas_call(solve_kernel, out_shape=jax.ShapeDtypeStruct((MGROUPS, col...  44.7 us
    pallas_call x1, Pallas kernels, exchange(): pl.pallas_call(exchange_kernel, out_shape=jax.ShapeDtypeStruct((blocks, X...  36.2 us
    all_to_all x1, starting transfers between devices, per_device(): lax.all_to_all(shaped, 'expert', split_axis=2, concat_axis=0, tiled=True)  8.76 us
    convert_element_type x1, local copies, waits for them, and re-layouts, per_device(): moved = jnp.einsum('bid,bin->bdn', down_weight.reshape(blocks, NB, width)...  5.95 us
    dot_general x1, matrix products, per_device(): jnp.einsum('bid,bin->bdn', down_weight.reshape(blocks, NB, width), select...  5.03 us
  transfers between devices with their start and end apart: 1, of which 0 were waited for; matrix products, arithmetic and copies ran while one was open for 1% of the time, Pallas kernels for 68%

profile of v1, /device:TPU:1, one launch (start us, length us, event | category | flops | bytes accessed | tf_op | source)
XLA Modules:
  0.0 222.0 jit_solution(11340408973142940027)
XLA Ops:
  0.0 0.7 broadcast_subtract_fusion
  0.8 5.0 %fusion = bf16[2,7168,128]{1,2,0:T(8,128)(2,1)} fusion(bf16[2,128,7168]{2,1,0:T(8,128)(2,1)} %bitcast.17, s32[2,128]{1,0:T(2,128)S(1)} %broadcast_subtract_fusion), kind=kOutput, calls=%fused_computation.1 | convolution fusion | flops 471629824 | bytes 7341056 | tf_op jit(solution)/shard_map/bid,bin->bdn/dot_general | solution.py:539
  5.8 6.0 %copy.13 = bf16[2,7168,128]{2,1,0:T(8,128)(2,1)} copy(bf16[2,7168,128]{1,2,0:T(8,128)(2,1)} %fusion) | data formatting | bytes 7340032 | tf_op jit(solution)/shard_map/convert_element_type | solution.py:541
  11.7 4.3 %copy.14 = bf16[1,2,32,224,128]{4,3,1,0,2:T(8,128)(2,1)} copy(bf16[1,2,32,224,128]{4,3,2,1,0:T(8,128)(2,1)} %bitcast.16) | data formatting | bytes 7340032 | tf_op jit(solution)/shard_map/reshape | solution.py:543
  16.1 0.0 copy-start.1
  16.1 0.0 copy-start
  16.1 8.8 %all-to-all-start = ((bf16[1,2,32,224,128]{4,3,1,0,2:T(8,128)(2,1)}), bf16[1,2,32,224,128]{4,3,1,0,2:T(8,128)(2,1)}, u32[]{:S(2)}, u32[]{:S(2)}) async-start(bf16[1,2,32,224,128]{4,3,1,0,2:T(8,128)(2,1)} %copy.14), calls=%async_computation | async-start | bytes 7340032 | tf_op jit(solution)/shard_map/all_to_all | solution.py:544
  24.8 0.0 copy-done.1
  24.9 0.0 copy-done
  24.9 0.7 fusion.3.tok_ref
  25.5 114.8 %gather_grams.1.part_ref = f32[2,2,128,128]{3,2,1,0:T(8,128)} custom-call(bf16[8,7296]{1,0:T(8,128)(2,1)} %fusion.3.tok_ref, bf16[7168,256]{1,0:T(8,128)(2,1)} %bitcast.18, bf16[7168,256]{1,0:T(8,128)(2,1)} %bitcast.19), custom_call_target="tpu_custom_call" | custom-call | tf_op jit(solution)/shard_map/gather_grams/pallas_call | solution.py:233
  140.3 0.6 fusion.2.selector_ref
  141.0 36.2 %exchange_grams.1 = f32[2,4,4,2,128,128]{5,4,3,2,1,0:T(8,128)} custom-call(f32[2,2,128,128]{3,2,1,0:T(8,128)} %gather_grams.1.part_ref, bf16[2,128,128]{2,1,0:T(8,128)(2,1)} %fusion.2.selector_ref), custom_call_target="tpu_custom_call" | custom-call | tf_op jit(solution)/shard_map/exchange_grams/pallas_call | solution.py:512
  177.2 0.0 all-to-all-done
  177.2 44.7 %solve.1 = bf16[8,224,256]{2,1,0:T(8,128)(2,1)} custom-call(s32[32]{0:T(128)} %group_of.1, f32[2,32,128,128]{3,2,1,0:T(8,128)} %bitcast.15, bf16[32,2,224,128]{3,2,1,0:T(8,128)(2,1)} %bitcast.9.moved_ref), custom_call_target="tpu_custom_call" | custom-call | tf_op jit(solution)/shard_map/solve/pallas_call | solution.py:361
  (2 shorter events, 0.0 us)
Async XLA Ops:
  16.1 8.8 %copy-start.1 = (s32[8,8]{1,0:T(8,128)S(1)}, s32[8,8]{1,0:T(8,128)}, u32[]{:S(2)}) copy-start(s32[8,8]{1,0:T(8,128)} %param.8) | copy-start | bytes 772
  16.1 8.8 %copy-start = (bf16[8,7168]{1,0:T(8,128)(2,1)S(1)}, bf16[8,7168]{1,0:T(8,128)(2,1)}, u32[]{:S(2)}) copy-start(bf16[8,7168]{1,0:T(8,128)(2,1)} %param.7) | copy-start | bytes 344068
  16.1 161.1 %all-to-all-start = ((bf16[1,2,32,224,128]{4,3,1,0,2:T(8,128)(2,1)}), bf16[1,2,32,224,128]{4,3,1,0,2:T(8,128)(2,1)}, u32[]{:S(2)}, u32[]{:S(2)}) async-start(bf16[1,2,32,224,128]{4,3,1,0,2:T(8,128)(2,1)} %copy.14), calls=%async_computation | async-start | bytes 7340032 | tf_op jit(solution)/shard_map/all_to_all | solution.py:544

commit v2 on v1

v2 whole, which is shorter than its diff:
```python
from functools import partial

import jax
import jax.numpy as jnp
from jax import lax
from jax.experimental import pallas as pl
from jax.experimental.pallas import tpu as pltpu
from jax.sharding import PartitionSpec as P

NB = 128
F32 = jnp.float32
BF16 = jnp.bfloat16
MESH = pl.DeviceIdType.MESH
XN, YN, ZN = 4, 4, 8
SIZES = {"x": XN, "y": YN, "z": ZN}
ORDERS = ("zyx", "zxy", "yxz")


def place(x, y, core):
    return (x * YN + y) * 2 + core


def offsets(n):
    listed = [0]
    for d in range(1, n // 2):
        listed += [-d, d]
    return listed + [n // 2]


def last_ways(stage, color, n, index):
    if stage == 0:
        return (color % 2,)
    return ((0, 1, 1, 0)[index % 4],)


def transfers():
    found = {}
    for color, order in enumerate(ORDERS):
        for stage, axis in enumerate(order):
            n = SIZES[axis]
            pieces = (None,) if stage == 0 else tuple(offsets(SIZES[order[stage - 1]]))
            for step in range(1, n // 2 + 1):
                for index, piece in enumerate(pieces):
                    ways = (0, 1) if step < n // 2 else last_ways(stage, color, n, index)
                    for way in ways:
                        found[color, stage, way, step, piece] = None
    return found


def arrivals(tasks, color, stage, offset):
    if offset == 0:
        if stage == 0:
            return set()
        below = SIZES[ORDERS[color][stage - 1]]
        return set().union(*(arrivals(tasks, color, stage - 1, d) for d in offsets(below)))
    return {
        t for t in tasks
        if t[0] == color and t[1] == stage and t[3] == abs(offset)
        and (abs(offset) == SIZES[ORDERS[color][stage]] // 2 or t[2] == (0 if offset < 0 else 1))
    }


def schedule(chunks, depth=4.0, shallow=-0.5):
    tasks = transfers()
    needs = {}
    for t in tasks:
        color, stage, way, step, piece = t
        if step > 1:
            needs[t] = {(color, stage, way, step - 1, piece)}
        else:
            needs[t] = arrivals(tasks, color, stage - 1, piece) if stage else set()
    takes = {}
    for color, order in enumerate(ORDERS):
        for d in offsets(SIZES[order[2]]):
            takes["take", color, d] = arrivals(tasks, color, 2, d)
    fill = [("chunk", i) for i in range(chunks)]
    rate, delay = 39e-3 / 0.047, 2.0
    now, busy, landed, waited, plan = 0.0, {}, {}, set(), []

    def flush(need):
        for t in sorted(need - waited, key=lambda t: landed[t]):
            plan.append(("wait", t))
            waited.add(t)

    def urgency(t):
        return (t[1], t[3], 0 if t[4] is None else abs(t[4]), t[0], t[2])

    todo = sorted(tasks, key=urgency)
    while todo or takes:
        ready = [t for t in todo if all(landed.get(d, 1e9) <= now for d in needs[t])]
        queue = []
        for t in ready:
            color, stage, way, step, piece = t
            link = (ORDERS[color][stage], way)
            size = 1 if stage < 2 else SIZES[ORDERS[color][0]]
            urgent = any(u[1] < 2 and (ORDERS[u[0]][u[1]], u[2]) == link for u in todo)
            if stage == 2 and busy.get(link, 0.0) - now > (shallow if urgent else depth):
                continue
            busy[link] = max(busy.get(link, 0.0), now) + size * rate
            landed[t] = busy[link] + delay
            queue.append(t)
        for t in queue:
            flush(needs[t])
            plan.append(("start", t))
            todo.remove(t)
        if queue:
            continue
        open_takes = [k for k in takes if all(landed.get(d, 1e9) <= now for d in takes[k])] if now > 16 else []
        if open_takes:
            key = open_takes[0]
            flush(takes.pop(key))
            plan.append(key)
            now += 1.4 if key[1] < 2 else 1.0
        elif fill and now > 8:
            plan.append(fill.pop(0))
            now += 0.7
        else:
            later = [v for v in landed.values() if v > now] + ([16.001] if now <= 16 else [])
            now = min(later) if later else now + 0.5
    return plan + fill


def gather_kernel(part, width, tok_ref, gate_ref, up_ref, down_ref, perm_ref, merge_ref,
                  out_ref, moved_ref, plan_ref, bufx, bufy, bufz, weights, acc, lhs, down, moved,
                  send_sem, recv_sem, own_sem, wsem, wsend, wrecv, dsem, msem):
    expert = lax.axis_index("expert")
    z = lax.axis_index("group")
    core = lax.rem(expert, 2)
    y = lax.rem(lax.div(expert, 2), YN)
    x = lax.div(expert, 2 * YN)
    here = {"x": x, "y": y, "z": z}
    units = gate_ref.shape[1]
    blocks = units // NB
    experts = moved.shape[0]
    per_chunk = 4
    chunks = experts // per_chunk

    def shifted(axis, shift):
        return lax.rem(here[axis] + SIZES[axis] + shift, SIZES[axis])

    def device(axis, shift):
        at = dict(here)
        at[axis] = shifted(axis, shift)
        return (place(at["x"], at["y"], core), at["z"])

    partner = (place(x, y, 1 - core), z)
    bufs = (bufx, bufy, bufz)
    columns = (0, part, 2 * part)

    load_down = pltpu.make_async_copy(down_ref, down, dsem)
    load_down.start()
    barrier = pltpu.get_barrier_semaphore()
    neighbours = [device(a, s) for a in "xyz" for s in (1, -1)] + [partner]
    for other in neighbours:
        pl.semaphore_signal(barrier, inc=1, device_id=other, device_id_type=MESH)
    pl.semaphore_wait(barrier, len(neighbours))

    numbers = {t: i for i, t in enumerate(transfers())}

    def piece_ref(color, stage, offset, piece):
        order = ORDERS[color]
        buf = bufs[color]
        if stage == 0:
            return buf.at[here[order[2]], here[order[1]], shifted(order[0], offset)]
        if stage == 1:
            return buf.at[here[order[2]], shifted(order[1], offset), shifted(order[0], piece)]
        return buf.at[shifted(order[2], offset), shifted(order[1], piece)]

    started = {}

    def start(task):
        color, stage, way, step, piece = task
        sign = 1 - 2 * way
        dst = piece_ref(color, stage, -sign * (step - 1), piece)
        first = step == 1 and (stage == 0 or (stage == 1 and piece == 0))
        src = tok_ref.at[:, pl.ds(columns[color], part)] if first else dst
        i = numbers[task]
        copy = pltpu.make_async_remote_copy(
            src_ref=src,
            dst_ref=dst,
            send_sem=send_sem.at[i],
            recv_sem=recv_sem.at[i],
            device_id=device(ORDERS[color][stage], sign),
            device_id_type=MESH,
        )
        copy.start()
        started[task] = copy

    own = []
    for color in range(3):
        copy = pltpu.make_async_copy(
            tok_ref.at[:, pl.ds(columns[color], part)], piece_ref(color, 0, 0, None), own_sem.at[color]
        )
        copy.start()
        own.append(copy)
    moves = []

    def move_weights():
        for j, ref in enumerate((gate_ref, up_ref)):
            local = pltpu.make_async_copy(ref, weights.at[core * 2 + j], wsem.at[j])
            local.start()
            remote = pltpu.make_async_remote_copy(
                src_ref=ref,
                dst_ref=weights.at[core * 2 + j],
                send_sem=wsend.at[j],
                recv_sem=wrecv.at[j],
                device_id=partner,
                device_id_type=MESH,
            )
            remote.start()
            moves.append((local, remote))

    def multiply(rows, depth, first_row, color, plane):
        def per_column(n, carry):
            w = weights[n, pl.ds(first_row, depth), :]
            value = jnp.dot(lhs[0:rows, 0:depth], w, preferred_element_type=F32)
            if color == 0:
                acc[n, plane] += value.reshape(YN, ZN, 8, units)
            elif color == 1:
                acc[n, :, plane] += value.reshape(XN, ZN, 8, units)
            else:
                acc[n, :, :, plane] += value.reshape(XN, YN, 8, units)
            return carry

        lax.fori_loop(0, 4, per_column, 0)

    def take(color, offset):
        plane = shifted(ORDERS[color][2], offset)
        depth = part if color < 2 else width - 2 * part
        rows = 256 if color < 2 else 128
        value = bufs[color][plane, :, :, :, 0:depth].astype(F32)
        lhs[0:rows, 0:depth] = value.reshape(rows, depth).astype(BF16)
        multiply(rows, depth, columns[color], color, plane)

    unit_rows = lax.broadcasted_iota(jnp.int32, (NB, NB), 0)
    span = per_chunk * (width // experts)
    writes = []

    def chunk(i):
        for b in range(blocks):
            within = perm_ref[0:1, b * NB : (b + 1) * NB] - (z * units + b * NB)
            selector = (unit_rows == within).astype(F32).astype(BF16)
            piece = down[b * NB : (b + 1) * NB, i * span : (i + 1) * span]
            turned = lax.dot_general(piece, selector, (((0,), (0,)), ((), ())), preferred_element_type=F32)
            moved[i * per_chunk : (i + 1) * per_chunk, b] = turned.astype(BF16).reshape(per_chunk, span // per_chunk, NB)
        copy = pltpu.make_async_copy(
            moved.at[pl.ds(i * per_chunk, per_chunk)], moved_ref.at[pl.ds(i * per_chunk, per_chunk)], msem.at[i]
        )
        copy.start()
        writes.append(copy)

    order = schedule(chunks)
    begun = False
    settled = False
    for action, *rest in order:
        if action == "start":
            if not settled and rest[0][1] > 0:
                for copy in own:
                    copy.wait()
                settled = True
            start(rest[0])
        elif not begun:
            move_weights()
            acc[...] = jnp.zeros_like(acc)
            begun = True
        if action == "wait":
            started[rest[0]].wait_recv()
        elif action == "chunk":
            if rest[0] == 0:
                load_down.wait()
            chunk(rest[0])
        elif action == "take":
            if moves[0] is not None:
                for local, remote in moves:
                    local.wait()
                    remote.wait_recv()
                sent = [remote for _, remote in moves]
                moves[0] = None
            take(*rest)

    out_ref[...] = jnp.zeros_like(out_ref)
    spare = width - 2 * part

    def finish(i, carry):
        px, p = lax.div(i, 2), lax.rem(i, 2)
        named = (place(x, y, 0) + p).astype(F32)
        gate = acc[2 * p, px].reshape(256, units)
        up = acc[2 * p + 1, px].reshape(256, units)
        listed = jnp.concatenate(
            [bufz[:, px, py, :, spare : spare + NB].astype(F32).reshape(ZN * 8, NB) for py in range(YN)], axis=0
        )
        chosen = jnp.max(jnp.where(listed == named, 1.0, 0.0), axis=1, keepdims=True)
        value = gate / (1.0 + jnp.exp(-gate)) * up
        hidden = jnp.where(chosen > 0.5, value, 0.0).astype(BF16)
        for b in range(blocks):
            piece = hidden[:, b * NB : (b + 1) * NB]
            out_ref[p, b] += lax.dot_general(piece, piece, (((0,), (0,)), ((), ())), preferred_element_type=F32)
        return carry

    lax.fori_loop(0, 2 * XN, finish, 0)

    count = merge_ref.shape[1]
    ids = lax.broadcasted_iota(jnp.int32, (count, count), 0).astype(F32)
    lanes = lax.broadcasted_iota(jnp.int32, (count, count), 1).astype(F32)
    across = jnp.broadcast_to(merge_ref[0:1, :].astype(F32), (count, count))
    down_way = jnp.sum(jnp.where(ids == lanes, across, 0.0), axis=1, keepdims=True)
    before = (across < down_way) | ((across == down_way) & (lanes < ids))
    rank = jnp.sum(jnp.where(before, 1.0, 0.0), axis=1, keepdims=True)
    here_rank = rank == lanes
    after_rank = rank == lanes - 1.0
    listed = jnp.sum(jnp.where(here_rank, ids, 0.0), axis=0, keepdims=True)
    own_group = jnp.sum(jnp.where(here_rank, down_way, 0.0), axis=0, keepdims=True)
    last_group = jnp.sum(jnp.where(after_rank, down_way + 1.0, 0.0), axis=0, keepdims=True) - 1.0
    keep = jnp.where(own_group == last_group, 1.0, 0.0)
    ends = jnp.sum(jnp.where(down_way <= lanes, 1.0, 0.0), axis=0, keepdims=True) - 1.0
    plan_ref[...] = jnp.concatenate([listed, keep, ends], axis=0).astype(jnp.int32)

    for copy in started.values():
        copy.wait_send()
    for remote in sent:
        remote.wait_send()
    for copy in writes:
        copy.wait()


def gather_grams(tokens, routes, gate_weight, up_weight, down_weight, neuron_perm, merge_group):
    rows, width = tokens.shape
    units = gate_weight.shape[1]
    blocks = units // NB
    experts = merge_group.shape[0]
    listed = jnp.pad(routes.astype(BF16), ((0, 0), (0, NB - routes.shape[1])), constant_values=-1)
    wide = jnp.concatenate([tokens, listed], axis=1)
    part = (width + NB) // 3
    number = len(transfers())
    moved_shape = (experts, blocks, width // experts, NB)
    return pl.pallas_call(
        partial(gather_kernel, part, width),
        out_shape=(
            jax.ShapeDtypeStruct((2, blocks, NB, NB), F32),
            jax.ShapeDtypeStruct(moved_shape, BF16),
            jax.ShapeDtypeStruct((3, experts), jnp.int32),
        ),
        in_specs=[pl.BlockSpec(memory_space=pl.ANY)] * 4 + [pl.BlockSpec(memory_space=pltpu.VMEM)] * 2,
        out_specs=(
            pl.BlockSpec(memory_space=pltpu.VMEM),
            pl.BlockSpec(memory_space=pl.ANY),
            pl.BlockSpec(memory_space=pltpu.VMEM),
        ),
        scratch_shapes=[
            pltpu.VMEM((XN, YN, ZN, 8, part), BF16),
            pltpu.VMEM((YN, XN, ZN, 8, part), BF16),
            pltpu.VMEM((ZN, XN, YN, 8, part), BF16),
            pltpu.VMEM((4, width, units), BF16),
            pltpu.VMEM((4, XN, YN, ZN, 8, units), F32),
            pltpu.VMEM((256, part), BF16),
            pltpu.VMEM((units, width), BF16),
            pltpu.VMEM(moved_shape, BF16),
            pltpu.SemaphoreType.DMA((number,)),
            pltpu.SemaphoreType.DMA((number,)),
            pltpu.SemaphoreType.DMA((3,)),
            pltpu.SemaphoreType.DMA((2,)),
            pltpu.SemaphoreType.DMA((2,)),
            pltpu.SemaphoreType.DMA((2,)),
            pltpu.SemaphoreType.DMA,
            pltpu.SemaphoreType.DMA((8,)),
        ],
        compiler_params=pltpu.CompilerParams(collective_id=0, has_side_effects=True, vmem_limit_bytes=60 * 1024 * 1024),
        name="gather_grams",
    )(wide, gate_weight, up_weight, down_weight, neuron_perm, merge_group[None, :])


MGROUPS = 8
OFF_WEIGHT = 0.75
RIDGE = 1e-05
LOW = 16
BATCH = 4
HIGH = NB // LOW


def split_two(value):
    high = value.astype(BF16)
    return high, (value - high.astype(F32)).astype(BF16)


def dot3(left, right, contract):
    lh, ll = split_two(left)
    rh, rl = split_two(right)
    dims = (((1,), (contract,)), ((), ()))
    part = partial(lax.dot_general, dimension_numbers=dims, preferred_element_type=F32)
    return part(lh, rh) + part(lh, rl) + part(ll, rh)


def dot_exact(value, one_hot, value_left, contract):
    first = value.astype(BF16)
    rest = value - first.astype(F32)
    second = rest.astype(BF16)
    third = (rest - second.astype(F32)).astype(BF16)
    dims = (((contract,), (0,)), ((), ())) if value_left else (((0,), (contract,)), ((), ()))
    total = None
    for part in (first, second, third):
        pair = (part, one_hot) if value_left else (one_hot, part)
        term = lax.dot_general(*pair, dims, preferred_element_type=F32)
        total = term if total is None else total + term
    return total


def regroup(state, lanes):
    for bit in (1, 2, 4, 8):
        low = (lanes & bit) == 0
        for m in range(LOW):
            if m & bit:
                continue
            first, second = state[m], state[m | bit]
            state[m] = jnp.where(low, first, pltpu.roll(second, bit, 1))
            state[m | bit] = jnp.where(low, pltpu.roll(first, NB - bit, 1), second)


def eliminate(state, rows, lanes):
    def prepare(q, g):
        k = g * LOW + q
        pick = g * LOW + (lanes & (LOW - 1))
        row = jnp.take_along_axis(state[q], pick, axis=1, mode="promise_in_bounds")
        at_pivot = jnp.broadcast_to(state[q, pl.ds(k, 1), :], (8, NB))
        pivot = jnp.take_along_axis(at_pivot, pick[0:8], axis=1, mode="promise_in_bounds")
        inverse = (1.0 / pivot)[0:1]
        return (row + (rows == k).astype(F32)) * inverse

    for q in range(LOW):

        def step(g, scaled):
            k = g * LOW + q
            column = state[q, pl.ds(k, 1), :]
            column = jnp.where(lanes[0:1] >= (g + 1) * LOW, column, 0.0)
            state[q] = state[q] - column * scaled
            following = prepare(q, jnp.minimum(g + 1, HIGH - 1))
            for later in range(q + 1, LOW):
                state[later] = state[later] - state[later, pl.ds(k, 1), :] * scaled
            return following

        lax.fori_loop(0, HIGH, step, prepare(q, 0))


def solve_kernel(part_ref, perm_ref, plan_ref, moved_ref, out_ref, gram_ref, inbox, spread, runs, state, terms, scales,
                 send_sem, recv_sem, relay_send, relay_recv, pair_sem, all_send, all_recv, own_sem):
    expert = lax.axis_index("expert")
    z = lax.axis_index("group")
    core = lax.rem(expert, 2)
    y = lax.rem(lax.div(expert, 2), YN)
    x = lax.div(expert, 2 * YN)
    partner = (place(x, y, 1 - core), z)
    blocks = part_ref.shape[1]
    units = blocks * NB
    experts = spread.shape[0]
    rows = lax.broadcasted_iota(jnp.int32, (NB, NB), 0)
    lanes = lax.broadcasted_iota(jnp.int32, (NB, NB), 1)
    same = rows == lanes

    def device(axis, shift):
        if axis == "x":
            return (place(lax.rem(x + XN + shift, XN), y, core), z)
        return (place(x, lax.rem(y + YN + shift, YN), core), z)

    others = [(dx, dy, dc) for dx in range(XN) for dy in range(YN) for dc in range(2) if dx or dy or dc]

    def other(dx, dy, dc):
        return place(lax.rem(x + dx, XN), lax.rem(y + dy, YN), lax.rem(core + dc, 2))

    barrier = pltpu.get_barrier_semaphore()
    for shift in others:
        pl.semaphore_signal(barrier, inc=1, device_id=(other(*shift), z), device_id_type=MESH)
    pl.semaphore_wait(barrier, len(others))

    swap = pltpu.make_async_remote_copy(
        src_ref=part_ref.at[1 - core],
        dst_ref=inbox,
        send_sem=pair_sem.at[0],
        recv_sem=pair_sem.at[1],
        device_id=partner,
        device_id_type=MESH,
    )
    swap.start()
    axes = (("x", x), ("y", y))
    swap.wait_recv()
    for b in range(blocks):
        selector = (rows == perm_ref[0:1, b * NB : (b + 1) * NB] - (z * units + b * NB)).astype(F32).astype(BF16)
        summed = part_ref[core, b] + inbox[b]
        turned = dot_exact(summed, selector, False, 0)
        gram_ref[b, x, y, core] = dot_exact(turned, selector, True, 1)

    def unit(b, stage, pos, half=None):
        along = axes[b] if stage == 0 else axes[1 - b]
        if stage == 0:
            lead = (b, pos, y, core) if along[0] == "x" else (b, x, pos, core)
            return gram_ref.at[lead + ((pl.ds(half * (NB // 2), NB // 2),) if half is not None else ())]
        ring = pl.ds(0, XN) if half is None else pl.ds(half * (XN // 2), XN // 2)
        lead = (b, pos, ring, core) if along[0] == "x" else (b, ring, pos, core)
        return gram_ref.at[lead]

    started = {}

    def start(b, stage, step):
        axis, pos = axes[b] if stage == 0 else axes[1 - b]
        for way, sign in ((0, 1), (1, -1)):
            half = way if step == 2 else None
            ref = unit(b, stage, lax.rem(pos + XN - sign * (step - 1), XN), half)
            copy = pltpu.make_async_remote_copy(
                src_ref=ref,
                dst_ref=ref,
                send_sem=send_sem.at[b, stage, way, step - 1],
                recv_sem=recv_sem.at[b, stage, way, step - 1],
                device_id=device(axis, sign),
                device_id_type=MESH,
            )
            copy.start()
            started[b, stage, way, step] = copy

    def arrive(b, stage, step):
        for way in (0, 1):
            started[b, stage, way, step].wait_recv()

    relays = []

    def relay(b, shift):
        axis, pos = axes[1 - b]
        ref = unit(b, 1, lax.rem(pos + shift, XN))
        copy = pltpu.make_async_remote_copy(
            src_ref=ref,
            dst_ref=ref,
            send_sem=relay_send.at[b, shift],
            recv_sem=relay_recv.at[b, shift],
            device_id=partner,
            device_id_type=MESH,
        )
        copy.start()
        relays.append(copy)

    spreads = []

    def spread_some(which):
        for i in which:
            to = other(*others[i])
            copy = pltpu.make_async_remote_copy(
                src_ref=moved_ref.at[to],
                dst_ref=spread.at[expert],
                send_sem=all_send.at[i],
                recv_sem=all_recv.at[i],
                device_id=(to, z),
                device_id_type=MESH,
            )
            copy.start()
            spreads.append(copy)

    for b in range(blocks):
        start(b, 0, 1)
    for b in range(blocks):
        arrive(b, 0, 1)
        start(b, 0, 2)
    for b in range(blocks):
        arrive(b, 0, 2)
        start(b, 1, 1)
    for b in range(blocks):
        relay(b, 0)
    for b in range(blocks):
        arrive(b, 1, 1)
        start(b, 1, 2)
    for b in range(blocks):
        relay(b, 1)
        relay(b, 3)
    spread_some(range(len(others)))
    own = pltpu.make_async_copy(moved_ref.at[expert], spread.at[expert], own_sem)
    own.start()
    for b in range(blocks):
        arrive(b, 1, 2)
        relay(b, 2)
    for copy in relays:
        copy.wait_recv()

    def gram_of(b, e):
        return gram_ref[b, lax.div(e, 2 * YN), lax.rem(lax.div(e, 2), YN), lax.rem(e, 2)]

    for b in range(blocks):

        def add_grams(i, run):
            for d in range(BATCH):
                j = i * BATCH + d
                run = run * plan_ref[1, j].astype(F32) + gram_of(b, plan_ref[0, j])
                runs[j, 0:NB, :] = run
            return run

        lax.fori_loop(0, experts // BATCH, add_grams, jnp.zeros((NB, NB), F32))
        for m in range(MGROUPS):
            summed = runs[plan_ref[2, m], 0:NB, :]
            diagonal = jnp.where(same, summed + RIDGE, 0.0)
            across = lax.rsqrt(jnp.sum(diagonal, axis=0, keepdims=True))
            down = lax.rsqrt(jnp.sum(diagonal, axis=1, keepdims=True))
            i = m * blocks + b
            scales[i] = jnp.broadcast_to(across, (8, NB))
            state[i] = jnp.where(same, diagonal, OFF_WEIGHT * summed) * down * across

    regroup(state, lanes)
    eliminate(state, rows, lanes)
    regroup(state, lanes)

    own.wait()
    for copy in spreads:
        copy.wait_recv()

    for b in range(blocks):

        def add_terms(i, run):
            made = []
            for d in range(BATCH):
                e = plan_ref[0, i * BATCH + d]
                high, low = split_two(gram_of(b, e))
                moved = spread[e, b]
                made.append(
                    jnp.dot(
                        jnp.concatenate([moved, moved], axis=1),
                        jnp.concatenate([high, low], axis=0),
                        preferred_element_type=F32,
                    )
                )
            for d in range(BATCH):
                run = run * plan_ref[1, i * BATCH + d].astype(F32) + made[d]
                runs[i * BATCH + d] = run
            return run

        lax.fori_loop(0, experts // BATCH, add_terms, jnp.zeros(runs.shape[1:], F32))
        for m in range(MGROUPS):
            terms[m * blocks + b] = runs[plan_ref[2, m]]

    turn_rows = (rows & (LOW - 1)) * HIGH + lax.shift_right_logical(rows, 4)
    turn_lanes = (lanes & (LOW - 1)) * HIGH + lax.shift_right_logical(lanes, 4)
    earlier = turn_rows < turn_lanes
    for m in range(MGROUPS):
        for b in range(blocks):
            i = m * blocks + b
            full = state[i]
            lower = jnp.where(earlier, full, jnp.where(same, 1.0, 0.0))
            inverse = 1.0 / jnp.sum(jnp.where(same, full, 0.0), axis=0, keepdims=True)
            scale = scales[i, 0:1, :]
            half = dot3(terms[i] * scale, lower, 0) * inverse
            merged = dot3(half, lower, 1) * scale
            out_ref[m, :, b * NB : (b + 1) * NB] = merged.astype(BF16)

    for copy in relays + spreads + list(started.values()):
        copy.wait_send()
    swap.wait_send()


def solve(partials, neuron_perm, plan, moved):
    experts, blocks, columns, _ = moved.shape
    systems = MGROUPS * blocks
    return pl.pallas_call(
        solve_kernel,
        out_shape=jax.ShapeDtypeStruct((MGROUPS, columns, blocks * NB), BF16),
        in_specs=[
            pl.BlockSpec(memory_space=pltpu.VMEM),
            pl.BlockSpec(memory_space=pltpu.VMEM),
            pl.BlockSpec(memory_space=pltpu.SMEM),
            pl.BlockSpec(memory_space=pl.ANY),
        ],
        out_specs=pl.BlockSpec(memory_space=pltpu.VMEM),
        scratch_shapes=[
            pltpu.VMEM((blocks, XN, YN, 2, NB, NB), F32),
            pltpu.VMEM((blocks, NB, NB), F32),
            pltpu.VMEM(moved.shape, BF16),
            pltpu.VMEM((experts, columns, NB), F32),
            pltpu.VMEM((systems, NB, NB), F32),
            pltpu.VMEM((systems, columns, NB), F32),
            pltpu.VMEM((systems, 8, NB), F32),
            pltpu.SemaphoreType.DMA((blocks, 2, 2, 2)),
            pltpu.SemaphoreType.DMA((blocks, 2, 2, 2)),
            pltpu.SemaphoreType.DMA((blocks, 4)),
            pltpu.SemaphoreType.DMA((blocks, 4)),
            pltpu.SemaphoreType.DMA((2,)),
            pltpu.SemaphoreType.DMA((experts - 1,)),
            pltpu.SemaphoreType.DMA((experts - 1,)),
            pltpu.SemaphoreType.DMA,
        ],
        compiler_params=pltpu.CompilerParams(collective_id=1, has_side_effects=True, vmem_limit_bytes=50 * 1024 * 1024),
        name="solve",
    )(partials, neuron_perm, plan, moved)


def per_device(tokens, routes, gate_weight, up_weight, down_weight, merge_group, neuron_perm):
    partials, moved, plan = gather_grams(
        tokens, routes, gate_weight[0], up_weight[0], down_weight[0], neuron_perm, merge_group
    )
    return jnp.swapaxes(solve(partials, neuron_perm, plan, moved), 1, 2)


def solution(mesh):
    in_specs = (
        P(("expert", "group"), None),
        P(("expert", "group"), None),
        P("expert", None, "group"),
        P("expert", None, "group"),
        P("expert", "group", None),
        P(),
        P("expert", "group"),
    )
    return jax.shard_map(
        per_device, mesh=mesh, in_specs=in_specs, out_specs=P(None, "group", "expert"), check_vma=False
    )
```

time: 222 us -> 172 us (0.77); the launches traced: 222 us -> 169 us
  Pallas kernels: 196 us -> 164 us
  starting transfers between devices: 8.76 us -> 0 us
  local copies, waits for them, and re-layouts: 10.3 us -> 2.54 us
  matrix products: 5.03 us -> 0 us
    pallas_call x2 -> x1, Pallas kernels: 151 us -> 77.4 us  [gather_grams(): pl.pallas_call(partial(gather_kernel, part, width), out_shape=(jax.ShapeD...]
    pallas_call x1, Pallas kernels: 44.7 us -> 86.6 us  [solve(): pl.pallas_call(solve_kernel, out_shape=jax.ShapeDtypeStruct((MGROUPS, col...]
    all_to_all x1 -> x0, starting transfers between devices: 8.76 us -> none  [per_device(): lax.all_to_all(shaped, 'expert', split_axis=2, concat_axis=0, tiled=True)]
    convert_element_type x1 -> x0, local copies, waits for them, and re-layouts: 5.95 us -> none  [per_device(): moved = jnp.einsum('bid,bin->bdn', down_weight.reshape(blocks, NB, width)...]
    dot_general x1 -> x0, matrix products: 5.03 us -> none  [per_device(): jnp.einsum('bid,bin->bdn', down_weight.reshape(blocks, NB, width), select...]
    reshape x1 -> x0, local copies, waits for them, and re-layouts: 4.34 us -> none  [per_device(): shaped = moved.reshape(1, blocks, experts, columns, NB)]
    unnamed x4 -> x7, local copies, waits for them, and re-layouts: 0.01 us -> 2.54 us
  transfers between devices with their start and end apart: 1 -> 0, of which waited for: 0 -> 0; matrix products, arithmetic and copies ran while one was open for 1% -> 0% of each run, Pallas kernels for 68% -> 0%
where the time goes in v2:
time: 172 us; the launch traced here: 169 us
  Pallas kernels  164 us (95%)
  local copies, waits for them, and re-layouts  2.54 us (1%)
  other arithmetic  2.24 us (1%)
    pallas_call x1, Pallas kernels, solve(): pl.pallas_call(solve_kernel, out_shape=jax.ShapeDtypeStruct((MGROUPS, col...  86.6 us
    pallas_call x1, Pallas kernels, gather_grams(): pl.pallas_call(partial(gather_kernel, part, width), out_shape=(jax.ShapeD...  77.4 us

profile of v2, /device:TPU:1, one launch (start us, length us, event | category | flops | bytes accessed | tf_op | source)
XLA Modules:
  0.0 168.8 jit_solution(4405557099269307435)
XLA Ops:
  0.0 0.7 convert_element_type.5
  0.7 1.6 fusion.1.tok_ref
  2.2 0.0 copy-start.1
  2.2 77.4 %gather_grams.1 = (f32[2,2,128,128]{3,2,1,0:T(8,128)}, bf16[32,2,224,128]{3,2,1,0:T(8,128)(2,1)}, s32[3,32]{1,0:T(4,128)}) custom-call(bf16[8,7296]{1,0:T(8,128)(2,1)} %fusion.1.tok_ref, bf16[7168,256]{1,0:T(8,128)(2,1)} %bitcast.6, bf16[7168,256]{1,0:T(8,128)(2,1)} %bitcast.7, bf16[256,7168]{1,0:T(8,128)(2,1)} %bitcast.8, s32[1,256]{1,0:T(1,128)} %perm_ref.3, ...), custom_call_target="tpu_custom_call" | custom-call | tf_op jit(solution)/shard_map/gather_grams/pallas_call | solution.py:336
  79.6 0.0 copy-done.1
  79.6 0.0 copy-start
  79.6 0.9 copy-done
  80.6 0.0 copy-start.2
  80.6 0.7 copy-done.2
  81.3 86.6 %solve.1 = bf16[8,224,256]{2,1,0:T(8,128)(2,1)S(1)} custom-call(f32[2,2,128,128]{3,2,1,0:T(8,128)S(1)} %copy-done, s32[1,256]{1,0:T(1,128)S(1)} %copy-done.1, s32[3,32]{1,0:T(4,128)S(1)} %copy-done.2, bf16[32,2,224,128]{3,2,1,0:T(8,128)(2,1)} %get-tuple-element.10.moved_ref), custom_call_target="tpu_custom_call" | custom-call | tf_op jit(solution)/shard_map/solve/pallas_call | solution.py:654
  167.9 0.9 copy.9
Async XLA Ops:
  2.2 77.4 %copy-start.1 = (s32[1,256]{1,0:T(1,128)S(1)}, s32[1,256]{1,0:T(1,128)}, u32[]{:S(2)}) copy-start(s32[1,256]{1,0:T(1,128)} %perm_ref.3) | copy-start | bytes 3076
  79.6 1.0 copy-start
  80.6 0.7 copy-start.2

commit v3 on v2

v3 whole, which is shorter than its diff:
```python
from functools import partial

import jax
import jax.numpy as jnp
from jax import lax
from jax.experimental import pallas as pl
from jax.experimental.pallas import tpu as pltpu
from jax.sharding import PartitionSpec as P

NB = 128
F32 = jnp.float32
BF16 = jnp.bfloat16
MESH = pl.DeviceIdType.MESH
XN, YN, ZN = 4, 4, 8
SIZES = {"x": XN, "y": YN, "z": ZN}
ORDERS = ("zyx", "zxy", "yxz")


def place(x, y, core):
    return (x * YN + y) * 2 + core


def offsets(n):
    listed = [0]
    for d in range(1, n // 2):
        listed += [-d, d]
    return listed + [n // 2]


def last_ways(stage, color, n, index):
    if stage == 0:
        return (color % 2,)
    return ((0, 1, 1, 0)[index % 4],)


def transfers():
    found = {}
    for color, order in enumerate(ORDERS):
        for stage, axis in enumerate(order):
            n = SIZES[axis]
            pieces = (None,) if stage == 0 else tuple(offsets(SIZES[order[stage - 1]]))
            for step in range(1, n // 2 + 1):
                for index, piece in enumerate(pieces):
                    ways = (0, 1) if step < n // 2 else last_ways(stage, color, n, index)
                    for way in ways:
                        found[color, stage, way, step, piece] = None
    return found


def arrivals(tasks, color, stage, offset):
    if offset == 0:
        if stage == 0:
            return set()
        below = SIZES[ORDERS[color][stage - 1]]
        return set().union(*(arrivals(tasks, color, stage - 1, d) for d in offsets(below)))
    return {
        t for t in tasks
        if t[0] == color and t[1] == stage and t[3] == abs(offset)
        and (abs(offset) == SIZES[ORDERS[color][stage]] // 2 or t[2] == (0 if offset < 0 else 1))
    }


def schedule(chunks, depth=4.0, shallow=-0.5):
    tasks = transfers()
    needs = {}
    for t in tasks:
        color, stage, way, step, piece = t
        if step > 1:
            needs[t] = {(color, stage, way, step - 1, piece)}
        else:
            needs[t] = arrivals(tasks, color, stage - 1, piece) if stage else set()
    takes = {}
    for color, order in enumerate(ORDERS):
        for d in offsets(SIZES[order[2]]):
            takes["take", color, d] = arrivals(tasks, color, 2, d)
    fill = [("chunk", i) for i in range(chunks)]
    rate, delay = 39e-3 / 0.047, 2.0
    now, busy, landed, waited, plan = 0.0, {}, {}, set(), []

    def flush(need):
        for t in sorted(need - waited, key=lambda t: landed[t]):
            plan.append(("wait", t))
            waited.add(t)

    def urgency(t):
        return (t[1], t[3], 0 if t[4] is None else abs(t[4]), t[0], t[2])

    todo = sorted(tasks, key=urgency)
    while todo or takes:
        ready = [t for t in todo if all(landed.get(d, 1e9) <= now for d in needs[t])]
        queue = []
        for t in ready:
            color, stage, way, step, piece = t
            link = (ORDERS[color][stage], way)
            size = 1 if stage < 2 else SIZES[ORDERS[color][0]]
            urgent = any(u[1] < 2 and (ORDERS[u[0]][u[1]], u[2]) == link for u in todo)
            if stage == 2 and busy.get(link, 0.0) - now > (shallow if urgent else depth):
                continue
            busy[link] = max(busy.get(link, 0.0), now) + size * rate
            landed[t] = busy[link] + delay
            queue.append(t)
        for t in queue:
            flush(needs[t])
            plan.append(("start", t))
            todo.remove(t)
        if queue:
            continue
        open_takes = [k for k in takes if all(landed.get(d, 1e9) <= now for d in takes[k])] if now > 16 else []
        if open_takes:
            key = open_takes[0]
            flush(takes.pop(key))
            plan.append(key)
            now += 1.4 if key[1] < 2 else 1.0
        elif fill and now > 8:
            plan.append(fill.pop(0))
            now += 0.7
        else:
            later = [v for v in landed.values() if v > now] + ([16.001] if now <= 16 else [])
            now = min(later) if later else now + 0.5
    return plan + fill


MGROUPS = 8
OFF_WEIGHT = 0.75
RIDGE = 1e-05
LOW = 16
BATCH = 4
EARLY = 16
HIGH = NB // LOW


def split_two(value):
    high = value.astype(BF16)
    return high, (value - high.astype(F32)).astype(BF16)


def dot3(left, right, contract):
    lh, ll = split_two(left)
    rh, rl = split_two(right)
    dims = (((1,), (contract,)), ((), ()))
    part = partial(lax.dot_general, dimension_numbers=dims, preferred_element_type=F32)
    return part(lh, rh) + part(lh, rl) + part(ll, rh)


def dot_exact(value, one_hot, value_left, contract):
    first = value.astype(BF16)
    rest = value - first.astype(F32)
    second = rest.astype(BF16)
    third = (rest - second.astype(F32)).astype(BF16)
    dims = (((contract,), (0,)), ((), ())) if value_left else (((0,), (contract,)), ((), ()))
    total = None
    for part in (first, second, third):
        pair = (part, one_hot) if value_left else (one_hot, part)
        term = lax.dot_general(*pair, dims, preferred_element_type=F32)
        total = term if total is None else total + term
    return total


def regroup(state, lanes):
    for bit in (1, 2, 4, 8):
        low = (lanes & bit) == 0
        for m in range(LOW):
            if m & bit:
                continue
            first, second = state[m], state[m | bit]
            state[m] = jnp.where(low, first, pltpu.roll(second, bit, 1))
            state[m | bit] = jnp.where(low, pltpu.roll(first, NB - bit, 1), second)


def eliminate(state, rows, lanes):
    def prepare(q, g):
        k = g * LOW + q
        pick = g * LOW + (lanes & (LOW - 1))
        row = jnp.take_along_axis(state[q], pick, axis=1, mode="promise_in_bounds")
        at_pivot = jnp.broadcast_to(state[q, pl.ds(k, 1), :], (8, NB))
        pivot = jnp.take_along_axis(at_pivot, pick[0:8], axis=1, mode="promise_in_bounds")
        inverse = (1.0 / pivot)[0:1]
        return (row + (rows == k).astype(F32)) * inverse

    for q in range(LOW):

        def step(g, scaled):
            k = g * LOW + q
            column = state[q, pl.ds(k, 1), :]
            column = jnp.where(lanes[0:1] >= (g + 1) * LOW, column, 0.0)
            state[q] = state[q] - column * scaled
            following = prepare(q, jnp.minimum(g + 1, HIGH - 1))
            for later in range(q + 1, LOW):
                state[later] = state[later] - state[later, pl.ds(k, 1), :] * scaled
            return following

        lax.fori_loop(0, HIGH, step, prepare(q, 0))


def merge_kernel(part, width, tok_ref, gate_ref, up_ref, down_ref, perm_ref, merge_ref, out_ref,
                 bufx, bufy, bufz, weights, acc, lhs, down, moved, part_ref, plan_rows, plan_ref,
                 gram_ref, inbox, spread, runs, state, terms, scales,
                 send_sem, recv_sem, own_sem, wsem, wsend, wrecv, dsem, plan_sem,
                 ring_send, ring_recv, relay_send, relay_recv, pair_sem, all_send, all_recv, keep_sem):
    expert = lax.axis_index("expert")
    z = lax.axis_index("group")
    core = lax.rem(expert, 2)
    y = lax.rem(lax.div(expert, 2), YN)
    x = lax.div(expert, 2 * YN)
    here = {"x": x, "y": y, "z": z}
    units = gate_ref.shape[1]
    blocks = units // NB
    experts = moved.shape[0]
    per_chunk = 4
    chunks = experts // per_chunk

    def shifted(axis, shift):
        return lax.rem(here[axis] + SIZES[axis] + shift, SIZES[axis])

    def device(axis, shift):
        at = dict(here)
        at[axis] = shifted(axis, shift)
        return (place(at["x"], at["y"], core), at["z"])

    partner = (place(x, y, 1 - core), z)
    bufs = (bufx, bufy, bufz)
    columns = (0, part, 2 * part)

    load_down = pltpu.make_async_copy(down_ref, down, dsem)
    load_down.start()
    barrier = pltpu.get_barrier_semaphore()
    others = [(dx, dy, dc) for dx in range(XN) for dy in range(YN) for dc in range(2) if dx or dy or dc]
    others = [others[(i * 13) % len(others)] for i in range(len(others))]

    def other(dx, dy, dc):
        return place(lax.rem(x + dx, XN), lax.rem(y + dy, YN), lax.rem(core + dc, 2))

    neighbours = [device("z", s) for s in (1, -1)] + [(other(*shift), z) for shift in others]
    for to in neighbours:
        pl.semaphore_signal(barrier, inc=1, device_id=to, device_id_type=MESH)
    pl.semaphore_wait(barrier, len(neighbours))

    numbers = {t: i for i, t in enumerate(transfers())}

    def piece_ref(color, stage, offset, piece):
        order = ORDERS[color]
        buf = bufs[color]
        if stage == 0:
            return buf.at[here[order[2]], here[order[1]], shifted(order[0], offset)]
        if stage == 1:
            return buf.at[here[order[2]], shifted(order[1], offset), shifted(order[0], piece)]
        return buf.at[shifted(order[2], offset), shifted(order[1], piece)]

    started = {}

    def start(task):
        color, stage, way, step, piece = task
        sign = 1 - 2 * way
        dst = piece_ref(color, stage, -sign * (step - 1), piece)
        first = step == 1 and (stage == 0 or (stage == 1 and piece == 0))
        src = tok_ref.at[:, pl.ds(columns[color], part)] if first else dst
        i = numbers[task]
        copy = pltpu.make_async_remote_copy(
            src_ref=src,
            dst_ref=dst,
            send_sem=send_sem.at[i],
            recv_sem=recv_sem.at[i],
            device_id=device(ORDERS[color][stage], sign),
            device_id_type=MESH,
        )
        copy.start()
        started[task] = copy

    own = []
    for color in range(3):
        copy = pltpu.make_async_copy(
            tok_ref.at[:, pl.ds(columns[color], part)], piece_ref(color, 0, 0, None), own_sem.at[color]
        )
        copy.start()
        own.append(copy)
    moves = []

    def move_weights():
        for j, ref in enumerate((gate_ref, up_ref)):
            local = pltpu.make_async_copy(ref, weights.at[core * 2 + j], wsem.at[j])
            local.start()
            remote = pltpu.make_async_remote_copy(
                src_ref=ref,
                dst_ref=weights.at[core * 2 + j],
                send_sem=wsend.at[j],
                recv_sem=wrecv.at[j],
                device_id=partner,
                device_id_type=MESH,
            )
            remote.start()
            moves.append((local, remote))

    def multiply(rows, depth, first_row, color, plane):
        def per_column(n, carry):
            w = weights[n, pl.ds(first_row, depth), :]
            value = jnp.dot(lhs[0:rows, 0:depth], w, preferred_element_type=F32)
            if color == 0:
                acc[n, plane] += value.reshape(YN, ZN, 8, units)
            elif color == 1:
                acc[n, :, plane] += value.reshape(XN, ZN, 8, units)
            else:
                acc[n, :, :, plane] += value.reshape(XN, YN, 8, units)
            return carry

        lax.fori_loop(0, 4, per_column, 0)

    def take(color, offset):
        plane = shifted(ORDERS[color][2], offset)
        depth = part if color < 2 else width - 2 * part
        rows = 256 if color < 2 else 128
        value = bufs[color][plane, :, :, :, 0:depth].astype(F32)
        lhs[0:rows, 0:depth] = value.reshape(rows, depth).astype(BF16)
        multiply(rows, depth, columns[color], color, plane)

    unit_rows = lax.broadcasted_iota(jnp.int32, (NB, NB), 0)
    span = per_chunk * (width // experts)

    def chunk(i):
        for b in range(blocks):
            within = perm_ref[0:1, b * NB : (b + 1) * NB] - (z * units + b * NB)
            selector = (unit_rows == within).astype(F32).astype(BF16)
            piece = down[b * NB : (b + 1) * NB, i * span : (i + 1) * span]
            turned = lax.dot_general(piece, selector, (((0,), (0,)), ((), ())), preferred_element_type=F32)
            moved[i * per_chunk : (i + 1) * per_chunk, b] = turned.astype(BF16).reshape(per_chunk, span // per_chunk, NB)

    spreads = []

    def spread_some(which):
        for i in which:
            to = other(*others[i])
            copy = pltpu.make_async_remote_copy(
                src_ref=moved.at[to],
                dst_ref=spread.at[expert],
                send_sem=all_send.at[i],
                recv_sem=all_recv.at[i],
                device_id=(to, z),
                device_id_type=MESH,
            )
            copy.start()
            spreads.append(copy)

    order = schedule(chunks)
    starts_left = len(numbers)
    begun = False
    settled = False
    for action, *rest in order:
        if action == "start":
            if not settled and rest[0][1] > 0:
                for copy in own:
                    copy.wait()
                settled = True
            start(rest[0])
            starts_left -= 1
            if starts_left == 0:
                spread_some(range(EARLY))
        elif not begun:
            move_weights()
            acc[...] = jnp.zeros_like(acc)
            begun = True
        if action == "wait":
            started[rest[0]].wait_recv()
        elif action == "chunk":
            if rest[0] == 0:
                load_down.wait()
            chunk(rest[0])
        elif action == "take":
            if moves[0] is not None:
                for local, remote in moves:
                    local.wait()
                    remote.wait_recv()
                sent = [remote for _, remote in moves]
                moves[0] = None
            take(*rest)

    part_ref[...] = jnp.zeros_like(part_ref)
    spare = width - 2 * part

    def finish(i, carry):
        px, p = lax.rem(i, XN), lax.rem(1 - core + lax.div(i, XN), 2)
        named = (place(x, y, 0) + p).astype(F32)
        gate = acc[2 * p, px].reshape(256, units)
        up = acc[2 * p + 1, px].reshape(256, units)
        listed = jnp.concatenate(
            [bufz[:, px, py, :, spare : spare + NB].astype(F32).reshape(ZN * 8, NB) for py in range(YN)], axis=0
        )
        chosen = jnp.max(jnp.where(listed == named, 1.0, 0.0), axis=1, keepdims=True)
        value = gate / (1.0 + jnp.exp(-gate)) * up
        hidden = jnp.where(chosen > 0.5, value, 0.0).astype(BF16)
        for b in range(blocks):
            piece = hidden[:, b * NB : (b + 1) * NB]
            part_ref[p, b] += lax.dot_general(piece, piece, (((0,), (0,)), ((), ())), preferred_element_type=F32)
        return carry

    lax.fori_loop(0, 2 * XN, finish, 0)
    swap = pltpu.make_async_remote_copy(
        src_ref=part_ref.at[1 - core],
        dst_ref=inbox,
        send_sem=pair_sem.at[0],
        recv_sem=pair_sem.at[1],
        device_id=partner,
        device_id_type=MESH,
    )
    swap.start()
    plan_rows[...] = jnp.zeros_like(plan_rows)
    count = merge_ref.shape[1]
    ids = lax.broadcasted_iota(jnp.int32, (count, count), 0).astype(F32)
    lanes = lax.broadcasted_iota(jnp.int32, (count, count), 1).astype(F32)
    across = jnp.broadcast_to(merge_ref[0:1, :].astype(F32), (count, count))
    down_way = jnp.sum(jnp.where(ids == lanes, across, 0.0), axis=1, keepdims=True)
    before = (across < down_way) | ((across == down_way) & (lanes < ids))
    rank = jnp.sum(jnp.where(before, 1.0, 0.0), axis=1, keepdims=True)
    here_rank = rank == lanes
    after_rank = rank == lanes - 1.0
    listed = jnp.sum(jnp.where(here_rank, ids, 0.0), axis=0, keepdims=True)
    own_group = jnp.sum(jnp.where(here_rank, down_way, 0.0), axis=0, keepdims=True)
    last_group = jnp.sum(jnp.where(after_rank, down_way + 1.0, 0.0), axis=0, keepdims=True) - 1.0
    keep = jnp.where(own_group == last_group, 1.0, 0.0)
    ends = jnp.sum(jnp.where(down_way <= lanes, 1.0, 0.0), axis=0, keepdims=True) - 1.0
    for i, row in enumerate((listed, keep, ends)):
        plan_rows[i : i + 1, 0:count] = row.astype(jnp.int32)
    plan_copy = pltpu.make_async_copy(plan_rows, plan_ref, plan_sem)
    plan_copy.start()


    rows = lax.broadcasted_iota(jnp.int32, (NB, NB), 0)
    lanes = lax.broadcasted_iota(jnp.int32, (NB, NB), 1)
    same = rows == lanes

    swap.wait_recv()
    for b in range(blocks):
        selector = (rows == perm_ref[0:1, b * NB : (b + 1) * NB] - (z * units + b * NB)).astype(F32).astype(BF16)
        summed = part_ref[core, b] + inbox[b]
        turned = dot_exact(summed, selector, False, 0)
        gram_ref[b, x, y, core] = dot_exact(turned, selector, True, 1)

    rings = ("xy", "yx")
    ring_tasks = {}
    for b in range(blocks):
        for stage in range(2):
            pieces = (None,) if stage == 0 else tuple(offsets(XN))
            for index, piece in enumerate(pieces):
                for step, ways in ((1, (0, 1)), (2, last_ways(stage, b, XN, index))):
                    for way in ways:
                        ring_tasks[b, stage, way, step, piece] = len(ring_tasks)

    def ring_ref(b, stage, offset, piece):
        first, second = rings[b]
        at = dict(here)
        if stage == 0:
            at[first] = shifted(first, offset)
        else:
            at[first], at[second] = shifted(first, piece), shifted(second, offset)
        return gram_ref.at[b, at["x"], at["y"], core]

    ringed = {}

    def ring_start(b, stage, step, piece=None):
        for way in (0, 1):
            key = (b, stage, way, step, piece)
            if key not in ring_tasks:
                continue
            sign = 1 - 2 * way
            ref = ring_ref(b, stage, -sign * (step - 1), piece)
            copy = pltpu.make_async_remote_copy(
                src_ref=ref,
                dst_ref=ref,
                send_sem=ring_send.at[ring_tasks[key]],
                recv_sem=ring_recv.at[ring_tasks[key]],
                device_id=device(rings[b][stage], sign),
                device_id_type=MESH,
            )
            copy.start()
            ringed[key] = copy

    def ring_arrive(b, stage, step, piece=None):
        for way in (0, 1):
            key = (b, stage, way, step, piece)
            if key in ringed:
                ringed[key].wait_recv()

    relays = []

    def relay(b, offset):
        first, second = rings[b]
        pos = shifted(second, offset)
        ref = gram_ref.at[b, :, pos, core] if first == "x" else gram_ref.at[b, pos, :, core]
        copy = pltpu.make_async_remote_copy(
            src_ref=ref,
            dst_ref=ref,
            send_sem=relay_send.at[b, offset % XN],
            recv_sem=relay_recv.at[b, offset % XN],
            device_id=partner,
            device_id_type=MESH,
        )
        copy.start()
        relays.append(copy)

    both = range(blocks)
    for b in both:
        ring_start(b, 0, 1)
    for b in both:
        ring_start(b, 1, 1, 0)
    for b in both:
        ring_arrive(b, 0, 1)
        ring_start(b, 0, 2)
        ring_start(b, 1, 1, -1)
        ring_start(b, 1, 1, 1)
    for b in both:
        ring_arrive(b, 1, 1, 0)
        ring_start(b, 1, 2, 0)
    for b in both:
        ring_arrive(b, 0, 2)
        ring_start(b, 1, 1, 2)
        relay(b, 0)
    for b in both:
        for piece in (-1, 1, 2):
            ring_arrive(b, 1, 1, piece)
            ring_start(b, 1, 2, piece)
    spread_some(range(EARLY, len(others)))
    own_rows = pltpu.make_async_copy(moved.at[expert], spread.at[expert], keep_sem)
    own_rows.start()
    for b in both:
        relay(b, -1)
        relay(b, 1)
    for b in both:
        for piece in offsets(XN):
            ring_arrive(b, 1, 2, piece)
        relay(b, 2)
    for copy in relays:
        copy.wait_recv()
    plan_copy.wait()

    def listed_at(i, j):
        return jnp.minimum(jnp.maximum(plan_ref[i, j], 0), experts - 1)

    def gram_of(b, e):
        return gram_ref[b, lax.div(e, 2 * YN), lax.rem(lax.div(e, 2), YN), lax.rem(e, 2)]

    for b in range(blocks):

        def add_grams(i, run):
            for d in range(BATCH):
                j = i * BATCH + d
                run = run * plan_ref[1, j].astype(F32) + gram_of(b, listed_at(0, j))
                runs[j, 0:NB, :] = run
            return run

        lax.fori_loop(0, experts // BATCH, add_grams, jnp.zeros((NB, NB), F32))
        for m in range(MGROUPS):
            summed = runs[listed_at(2, m), 0:NB, :]
            diagonal = jnp.where(same, summed + RIDGE, 0.0)
            across = lax.rsqrt(jnp.sum(diagonal, axis=0, keepdims=True))
            down = lax.rsqrt(jnp.sum(diagonal, axis=1, keepdims=True))
            i = m * blocks + b
            scales[i] = jnp.broadcast_to(across, (8, NB))
            state[i] = jnp.where(same, diagonal, OFF_WEIGHT * summed) * down * across

    regroup(state, lanes)
    eliminate(state, rows, lanes)
    regroup(state, lanes)

    own_rows.wait()
    for copy in spreads:
        copy.wait_recv()

    for b in range(blocks):

        def add_terms(i, run):
            made = []
            for d in range(BATCH):
                e = listed_at(0, i * BATCH + d)
                high, low = split_two(gram_of(b, e))
                moved = spread[e, b]
                made.append(
                    jnp.dot(
                        jnp.concatenate([moved, moved], axis=1),
                        jnp.concatenate([high, low], axis=0),
                        preferred_element_type=F32,
                    )
                )
            for d in range(BATCH):
                run = run * plan_ref[1, i * BATCH + d].astype(F32) + made[d]
                runs[i * BATCH + d] = run
            return run

        lax.fori_loop(0, experts // BATCH, add_terms, jnp.zeros(runs.shape[1:], F32))
        for m in range(MGROUPS):
            terms[m * blocks + b] = runs[listed_at(2, m)]

    turn_rows = (rows & (LOW - 1)) * HIGH + lax.shift_right_logical(rows, 4)
    turn_lanes = (lanes & (LOW - 1)) * HIGH + lax.shift_right_logical(lanes, 4)
    earlier = turn_rows < turn_lanes
    for m in range(MGROUPS):
        for b in range(blocks):
            i = m * blocks + b
            full = state[i]
            lower = jnp.where(earlier, full, jnp.where(same, 1.0, 0.0))
            inverse = 1.0 / jnp.sum(jnp.where(same, full, 0.0), axis=0, keepdims=True)
            scale = scales[i, 0:1, :]
            half = dot3(terms[i] * scale, lower, 0) * inverse
            merged = dot3(half, lower, 1) * scale
            out_ref[m, :, b * NB : (b + 1) * NB] = merged.astype(BF16)

    for copy in relays + spreads + sent + list(ringed.values()) + list(started.values()):
        copy.wait_send()
    swap.wait_send()


def merge(tokens, routes, gate_weight, up_weight, down_weight, neuron_perm, merge_group):
    rows, width = tokens.shape
    units = gate_weight.shape[1]
    blocks = units // NB
    experts = merge_group.shape[0]
    columns = width // experts
    systems = MGROUPS * blocks
    listed = jnp.pad(routes.astype(BF16), ((0, 0), (0, NB - routes.shape[1])), constant_values=-1)
    wide = jnp.concatenate([tokens, listed], axis=1)
    part = (width + NB) // 3
    number = len(transfers())
    moved_shape = (experts, blocks, columns, NB)
    dma = pltpu.SemaphoreType.DMA
    return pl.pallas_call(
        partial(merge_kernel, part, width),
        out_shape=jax.ShapeDtypeStruct((MGROUPS, columns, units), BF16),
        in_specs=[pl.BlockSpec(memory_space=pl.ANY)] * 4 + [pl.BlockSpec(memory_space=pltpu.VMEM)] * 2,
        out_specs=pl.BlockSpec(memory_space=pltpu.VMEM),
        scratch_shapes=[
            pltpu.VMEM((XN, YN, ZN, 8, part), BF16),
            pltpu.VMEM((YN, XN, ZN, 8, part), BF16),
            pltpu.VMEM((ZN, XN, YN, 8, part), BF16),
            pltpu.VMEM((4, width, units), BF16),
            pltpu.VMEM((4, XN, YN, ZN, 8, units), F32),
            pltpu.VMEM((256, part), BF16),
            pltpu.VMEM((units, width), BF16),
            pltpu.VMEM(moved_shape, BF16),
            pltpu.VMEM((2, blocks, NB, NB), F32),
            pltpu.VMEM((8, NB), jnp.int32),
            pltpu.SMEM((8, NB), jnp.int32),
            pltpu.VMEM((blocks, XN, YN, 2, NB, NB), F32),
            pltpu.VMEM((blocks, NB, NB), F32),
            pltpu.VMEM(moved_shape, BF16),
            pltpu.VMEM((experts, columns, NB), F32),
            pltpu.VMEM((systems, NB, NB), F32),
            pltpu.VMEM((systems, columns, NB), F32),
            pltpu.VMEM((systems, 8, NB), F32),
            dma((number,)),
            dma((number,)),
            dma((3,)),
            dma((2,)),
            dma((2,)),
            dma((2,)),
            dma,
            dma,
            dma((blocks * 15,)),
            dma((blocks * 15,)),
            dma((blocks, XN)),
            dma((blocks, XN)),
            dma((2,)),
            dma((experts - 1,)),
            dma((experts - 1,)),
            dma,
        ],
        compiler_params=pltpu.CompilerParams(collective_id=0, has_side_effects=True, vmem_limit_bytes=62 * 1024 * 1024),
        name="merge",
    )(wide, gate_weight, up_weight, down_weight, neuron_perm, merge_group[None, :])


def per_device(tokens, routes, gate_weight, up_weight, down_weight, merge_group, neuron_perm):
    merged = merge(tokens, routes, gate_weight[0], up_weight[0], down_weight[0], neuron_perm, merge_group)
    return jnp.swapaxes(merged, 1, 2)


def solution(mesh):
    in_specs = (
        P(("expert", "group"), None),
        P(("expert", "group"), None),
        P("expert", None, "group"),
        P("expert", None, "group"),
        P("expert", "group", None),
        P(),
        P("expert", "group"),
    )
    return jax.shard_map(
        per_device, mesh=mesh, in_specs=in_specs, out_specs=P(None, "group", "expert"), check_vma=False
    )
```

time: 172 us -> 151 us (0.88); the launches traced: 169 us -> 150 us
  Pallas kernels: 164 us -> 146 us
    pallas_call x2 -> x1, Pallas kernels: 164 us -> 146 us  [merge(): pl.pallas_call(partial(merge_kernel, part, width), out_shape=jax.ShapeDty...]
where the time goes in v3:
time: 151 us; the launch traced here: 150 us
  Pallas kernels  146 us (97%)
  other arithmetic  2.24 us (1%)
  local copies, waits for them, and re-layouts  2.16 us (1%)
    pallas_call x1, Pallas kernels, merge(): pl.pallas_call(partial(merge_kernel, part, width), out_shape=jax.ShapeDty...  146 us

profile of v3, /device:TPU:1, one launch (start us, length us, event | category | flops | bytes accessed | tf_op | source)
XLA Modules:
  0.0 150.3 jit_solution(13958741447184969101)
XLA Ops:
  0.0 0.7 convert_element_type.5
  0.7 1.6 %fusion.1.tok_ref = bf16[8,7296]{1,0:T(8,128)(2,1)} fusion(bf16[8,8]{1,0:T(8,128)(2,1)S(1)} %convert_element_type.5, bf16[8,7168]{1,0:T(8,128)(2,1)} %param.7), kind=kLoop, calls=%fused_computation.2 | loop fusion | flops 350208 | bytes 231552 | tf_op jit(solution)/shard_map/concatenate | solution.py:617
  2.2 145.9 %merge.1 = bf16[8,224,256]{2,1,0:T(8,128)(2,1)} custom-call(bf16[8,7296]{1,0:T(8,128)(2,1)} %fusion.1.tok_ref, bf16[7168,256]{1,0:T(8,128)(2,1)} %bitcast.6, bf16[7168,256]{1,0:T(8,128)(2,1)} %bitcast.7, bf16[256,7168]{1,0:T(8,128)(2,1)} %bitcast.8, s32[1,256]{1,0:T(1,128)} %perm_ref.1, s32[1,32]{1,0:T(1,128)} %bitcast.9), custom_call_target="tpu_custom_call" | custom-call | tf_op jit(solution)/shard_map/merge/pallas_call | solution.py:622
  148.2 2.2 %copy.9 = bf16[8,256,224]{1,2,0:T(8,128)(2,1)} copy(bf16[8,256,224]{1,2,0:T(8,128)(2,1)} %bitcast.5) | data formatting | bytes 1835008

commit v4 on v3

--- a/solution.py
+++ b/solution.py
@@ -125,7 +125,7 @@
 RIDGE = 1e-05
 LOW = 16
 BATCH = 4
-EARLY = 16
+EARLY = 13
 HIGH = NB // LOW
 
 

time: 151 us -> 146 us (0.967)
  Pallas kernels: 146 us -> 141 us
    pallas_call x1, Pallas kernels: 146 us -> 141 us  [merge(): pl.pallas_call(partial(merge_kernel, part, width), out_shape=jax.ShapeDty...]
where the time goes in v4:
time: 146 us
  Pallas kernels  141 us (97%)
  other arithmetic  2.24 us (2%)
  local copies, waits for them, and re-layouts  2.16 us (1%)
    pallas_call x1, Pallas kernels, merge(): pl.pallas_call(partial(merge_kernel, part, width), out_shape=jax.ShapeDty...  141 us

profile of v4, /device:TPU:1, one launch (start us, length us, event | category | flops | bytes accessed | tf_op | source)
XLA Modules:
  0.0 145.8 jit_solution(15077569654662533897)
XLA Ops:
  0.0 0.7 convert_element_type.5
  0.7 1.6 %fusion.1.tok_ref = bf16[8,7296]{1,0:T(8,128)(2,1)} fusion(bf16[8,8]{1,0:T(8,128)(2,1)S(1)} %convert_element_type.5, bf16[8,7168]{1,0:T(8,128)(2,1)} %param.7), kind=kLoop, calls=%fused_computation.2 | loop fusion | flops 350208 | bytes 231552 | tf_op jit(solution)/shard_map/concatenate | solution.py:617
  2.2 141.4 %merge.1 = bf16[8,224,256]{2,1,0:T(8,128)(2,1)} custom-call(bf16[8,7296]{1,0:T(8,128)(2,1)} %fusion.1.tok_ref, bf16[7168,256]{1,0:T(8,128)(2,1)} %bitcast.6, bf16[7168,256]{1,0:T(8,128)(2,1)} %bitcast.7, bf16[256,7168]{1,0:T(8,128)(2,1)} %bitcast.8, s32[1,256]{1,0:T(1,128)} %perm_ref.1, s32[1,32]{1,0:T(1,128)} %bitcast.9), custom_call_target="tpu_custom_call" | custom-call | tf_op jit(solution)/shard_map/merge/pallas_call | solution.py:622
  143.6 2.2 %copy.9 = bf16[8,256,224]{1,2,0:T(8,128)(2,1)} copy(bf16[8,256,224]{1,2,0:T(8,128)(2,1)} %bitcast.5) | data formatting | bytes 1835008
